TPU v7x, 256 devices: a whole 4x4x8 slice. The times are simulated.
256 devices in a mesh: space: 64 (over z, y, core), event: 4 (over x).
Axes of the slice: x: 4, y: 4, z: 8, core: 2. Of those that a mesh axis runs over, the one named last changes fastest.
Arguments:
- rain: bfloat16 [4, 2, 256, 4, 128], P('event', None, 'space'), may hold values from 0.049804688 to 5
- hidden_init: bfloat16 [4, 256, 128, 128], P('event', 'space'), may hold values from -3 to 3
- cell_init: float32 [4, 256, 128, 128], P('event', 'space'), may hold values from -6 to 6
- land_mask: int32 [256, 128], P('space'), may hold values 0 or 1
- hidden_weight: bfloat16 [9, 128, 512], replicated, may hold values from -0.1875 to 0.1875
- rain_weight: bfloat16 [9, 4, 512], replicated, may hold values from -1 to 1
- gate_bias: float32 [512], replicated, may hold values from -3 to 3
- cotangent: float32 [4, 2, 256, 128, 128], P('event', None, 'space'), may hold values from -6 to 6
Outputs:
- final_hidden: bfloat16 [4, 256, 128, 128], P('event', 'space')
- hidden_grad: float32 [4, 256, 128, 128], P('event', 'space')
- hidden_weight_grad: float32 [9, 128, 512], replicated
- rain_weight_grad: float32 [9, 4, 512], replicated
- bias_grad: float32 [512], replicated
All inputs are finite; a program needn't handle non-finite values. No bound on the sum of `land_mask` on one device may be relied on, other than what follows from the above.
Results may differ from a plain program's by a relative error of at most 0.0034.
Values may be sent and summed in bfloat16 or wider, within the bound.
No kernel may reach another device: no remote copies, remote signals or barrier semaphores. Data moves between devices by JAX's collectives and lax.ppermute only.
A program may use at most 64 MiB of HBM per device.

v0:
```python
import jax
import jax.numpy as jnp
from jax import lax
from jax.sharding import PartitionSpec as P


def with_halo(x, sides, width):
    for axis, dim in sides:
        size, length = (lax.axis_size(axis), x.shape[dim])
        up = [(i, (i + 1) % size) for i in range(size - 1)]
        down = [(j, i) for i, j in up]
        last = lax.slice_in_dim(x, length - width, length, axis=dim)
        first = lax.slice_in_dim(x, 0, width, axis=dim)
        before = lax.ppermute(last, axis, up)
        after = lax.ppermute(first, axis, down)
        x = jnp.concatenate([before, x, after], axis=dim)
    return x


def forward_gates(hidden_pad, rain_pad, hidden_weight, rain_weight, gate_bias, height, breadth):
    channels = hidden_pad.shape[-1]
    inputs = rain_pad.shape[-1]
    count = hidden_pad.shape[0] * height * breadth
    totals = jnp.zeros((count, hidden_weight.shape[-1]), jnp.float32) + gate_bias[None, :]
    for row_off in range(3):
        for col_off in range(3):
            tap = 3 * row_off + col_off
            hidden_taps = hidden_pad[
                :, row_off : row_off + height, col_off : col_off + breadth, :
            ].reshape(-1, channels)
            rain_taps = rain_pad[
                :, row_off : row_off + height, col_off : col_off + breadth, :
            ].reshape(-1, inputs)
            totals = totals + jnp.dot(
                hidden_taps, hidden_weight[tap], preferred_element_type=jnp.float32
            )
            totals = totals + jnp.dot(
                rain_taps, rain_weight[tap], preferred_element_type=jnp.float32
            )
    return totals


def lstm_update(totals, cell_prev, mask_cells):
    channels = cell_prev.shape[-1]
    input_gate = jax.nn.sigmoid(totals[:, :channels])
    forget_gate = jax.nn.sigmoid(totals[:, channels : 2 * channels])
    output_gate = jax.nn.sigmoid(totals[:, 2 * channels : 3 * channels])
    candidate = jnp.tanh(totals[:, 3 * channels :])
    cell_new = forget_gate * cell_prev + input_gate * candidate
    hidden_new = mask_cells * output_gate * jnp.tanh(cell_new)
    return ((input_gate, forget_gate, output_gate, candidate), cell_new, hidden_new)


def gate_grads(gates, cell_prev, cell_new, mask_cells, grad_hidden, grad_cell):
    input_gate, forget_gate, output_gate, candidate = gates
    squash = jnp.tanh(cell_new)
    masked = grad_hidden * mask_cells
    grad_output = masked * squash
    grad_cell = grad_cell + masked * output_gate * (1.0 - squash * squash)
    gate_grad = jnp.concatenate(
        [
            grad_cell * candidate * input_gate * (1.0 - input_gate),
            grad_cell * cell_prev * forget_gate * (1.0 - forget_gate),
            grad_output * output_gate * (1.0 - output_gate),
            grad_cell * input_gate * (1.0 - candidate * candidate),
        ],
        axis=1,
    ).astype(jnp.bfloat16)
    return (gate_grad, grad_cell * forget_gate)


def weight_terms(hidden_pad, rain_pad, gate_grad, height, breadth):
    dims = (((0,), (0,)), ((), ()))
    channels = hidden_pad.shape[-1]
    inputs = rain_pad.shape[-1]
    hidden_terms = []
    rain_terms = []
    for row_off in range(3):
        for col_off in range(3):
            hidden_taps = hidden_pad[
                :, row_off : row_off + height, col_off : col_off + breadth, :
            ].reshape(-1, channels)
            rain_taps = rain_pad[
                :, row_off : row_off + height, col_off : col_off + breadth, :
            ].reshape(-1, inputs)
            hidden_terms.append(
                lax.dot_general(hidden_taps, gate_grad, dims, preferred_element_type=jnp.float32)
            )
            rain_terms.append(
                lax.dot_general(rain_taps, gate_grad, dims, preferred_element_type=jnp.float32)
            )
    return (jnp.stack(hidden_terms), jnp.stack(rain_terms))


def spread_back(grad_pad, hidden_weight, height, breadth):
    dims = (((1,), (1,)), ((), ()))
    gates_width = grad_pad.shape[-1]
    count = grad_pad.shape[0] * height * breadth
    total = jnp.zeros((count, hidden_weight.shape[1]), jnp.float32)
    for row_off in range(3):
        for col_off in range(3):
            tap = 3 * row_off + col_off
            piece = grad_pad[
                :, 2 - row_off : 2 - row_off + height, 2 - col_off : 2 - col_off + breadth, :
            ].reshape(-1, gates_width)
            total = total + lax.dot_general(
                piece, hidden_weight[tap], dims, preferred_element_type=jnp.float32
            )
    return total


def on_device(
    rain, hidden_init, cell_init, land_mask, hidden_weight, rain_weight, gate_bias, cotangent
):
    events, steps, height, inputs, breadth = rain.shape
    channels = hidden_init.shape[-1]
    gates_width = hidden_weight.shape[-1]
    mask_cells = land_mask.astype(jnp.float32)[None].reshape(-1, 1)
    col_spec = ((0, 0), (0, 0), (1, 1), (0, 0))
    hidden = hidden_init
    cell = cell_init.reshape(-1, channels)
    stored = []
    for step in range(steps):
        rain_rows, hidden_rows = (
            with_halo(rain[:, step], (("space", 1),), 1),
            with_halo(hidden, (("space", 1),), 1),
        )
        hidden_pad = jnp.pad(hidden_rows, col_spec)
        rain_pad = jnp.pad(jnp.transpose(rain_rows, (0, 1, 3, 2)), col_spec)
        totals = forward_gates(
            hidden_pad, rain_pad, hidden_weight, rain_weight, gate_bias, height, breadth
        )
        gates, cell_new, hidden_new = lstm_update(totals, cell, mask_cells)
        stored.append((hidden_pad, rain_pad, gates, cell, cell_new))
        cell = cell_new
        hidden = hidden_new.astype(jnp.bfloat16).reshape(events, height, breadth, channels)
    grad_hidden = cotangent[:, steps - 1].reshape(-1, channels)
    grad_cell = jnp.zeros((events * height * breadth, channels), jnp.float32)
    grad_w_hidden = jnp.zeros(hidden_weight.shape, jnp.float32)
    grad_w_rain = jnp.zeros(rain_weight.shape, jnp.float32)
    grad_bias = jnp.zeros((gates_width,), jnp.float32)
    for step in reversed(range(steps)):
        hidden_pad, rain_pad, gates, cell_prev, cell_new = stored[step]
        gate_grad, grad_cell = gate_grads(
            gates, cell_prev, cell_new, mask_cells, grad_hidden, grad_cell
        )
        hidden_terms, rain_terms = weight_terms(hidden_pad, rain_pad, gate_grad, height, breadth)
        grad_w_hidden = grad_w_hidden + hidden_terms
        grad_w_rain = grad_w_rain + rain_terms
        grad_bias = grad_bias + jnp.sum(gate_grad.astype(jnp.float32), axis=0)
        grad_rows = with_halo(
            gate_grad.reshape(events, height, breadth, gates_width), (("space", 1),), 1
        )
        grad_hidden = spread_back(jnp.pad(grad_rows, col_spec), hidden_weight, height, breadth)
        if step > 0:
            grad_hidden = grad_hidden + cotangent[:, step - 1].reshape(-1, channels)
    grad_w_hidden, grad_w_rain, grad_bias = lax.psum(
        (grad_w_hidden, grad_w_rain, grad_bias), ("space", "event")
    )
    return (
        hidden,
        grad_hidden.reshape(events, height, breadth, channels),
        grad_w_hidden,
        grad_w_rain,
        grad_bias,
    )


def solution(mesh):
    in_specs = (
        P("event", None, "space", None, None),
        P("event", "space", None, None),
        P("event", "space", None, None),
        P("space", None),
        P(),
        P(),
        P(),
        P("event", None, "space", None, None),
    )
    out_specs = (P("event", "space", None, None), P("event", "space", None, None), P(), P(), P())
    return jax.shard_map(
        on_device, mesh=mesh, in_specs=in_specs, out_specs=out_specs, check_vma=False
    )
```

profile of v0, /device:TPU:1, one launch (start us, length us, event | category | flops | bytes accessed | tf_op | source)
XLA Modules:
  0.0 369.6 jit_solution(11438842138366548018)
XLA Ops:
  7.2 0.7 slice_bitcast_fusion.7
  7.9 5.1 %collective-permute-start.7 = (bf16[1,1,4,128]{3,2,1,0:T(4,128)(2,1)S(1)}, bf16[1,1,4,128]{3,2,1,0:T(4,128)(2,1)S(1)}, u32[]{:S(2)}, u32[]{:S(2)}) collective-permute-start(bf16[1,1,4,128]{3,2,1,0:T(4,128)(2,1)S(1)} %get-tuple-element.74), channel_id=1, source_target_pairs={{4,0},{8,4},{12,8},{16,12},{20,16},{24,20},{28,24},{32,28},{36,32}... | collective-permute-start | bytes 3080 | tf_op jit(solution)/shard_map/ppermute | solution.py:15
  13.1 1.9 collective-permute-start.6
  15.0 2.4 collective-permute-start.3
  17.4 3.2 collective-permute-start.2
  20.6 0.8 fusion.274
  21.4 1.9 collective-permute-start.1
  23.3 1.1 fusion.270
  24.4 0.7 convert_bitcast_fusion
  25.1 3.6 collective-permute-start
  28.8 1.0 fusion.183
  37.5 1.9 collective-permute-start.5
  39.4 3.6 collective-permute-start.4
  50.0 0.8 multiply_convert_fusion.5
  51.5 1.9 collective-permute-start.9
  53.5 4.4 %collective-permute-start.8 = (bf16[1,1,128,512]{3,2,1,0:T(8,128)(2,1)S(1)}, bf16[1,1,128,512]{3,2,1,0:T(8,128)(2,1)S(1)}, u32[]{:S(2)}, u32[]{:S(2)}) collective-permute-start(bf16[1,1,128,512]{3,2,1,0:T(8,128)(2,1)S(1)} %get-tuple-element.45), channel_id=1, source_target_pairs={{0,4},{4,8},{8,12},{12,16},{16,20},{20,24},{24,28},{28,32},{32,36}... | collective-permute-start | bytes 393224 | tf_op jit(solution)/shard_map/ppermute | solution.py:14
  66.1 1.9 collective-permute-start.11
  68.1 3.6 collective-permute-start.10
  75.3 2.0 add.284
  77.5 0.7 add.285
  78.2 97.8 %psum.23 = f32[512]{0:T(512)} all-reduce(f32[512]{0:T(512)S(1)} %add.286), channel_id=1, replica_groups=mesh['space'=64,'event'=4] {'space','event'}, use_global_device_ids=true, to_apply=%region_4.5 | all-reduce | flops 512 | bytes 4096 | tf_op jit(solution)/shard_map/psum | solution.py:157
  179.1 1.0 fusion.24
  180.2 178.6 %all-reduce.9.cloned.1.call-done = (f32[9,128,512]{2,1,0:T(8,128)}, f32[9,4,512]{2,1,0:T(4,128)}) async-done(((f32[9,128,512]{2,1,0:T(8,128)}, f32[9,4,512]{2,1,0:T(4,128)}), (f32[9,128,512]{2,1,0:T(8,128)}, f32[9,4,512]{2,1,0:T(4,128)})) %all-reduce.9.cloned.1.call-update) | async-done | bytes 2433040 | tf_op jit(solution)/shard_map/psum | solution.py:157
  358.8 3.3 copy.50
  (140 shorter events, 30.6 us)
Async XLA Ops:
  7.2 22.7 %copy-start.3 = (bf16[9,4,512]{2,1,0:T(4,128)(2,1)S(1)}, bf16[9,4,512]{2,1,0:T(4,128)(2,1)}, u32[]{:S(2)}) copy-start(bf16[9,4,512]{2,1,0:T(4,128)(2,1)} %param.13) | copy-start | bytes 110596
  7.2 351.6 %all-reduce.9.cloned.1.call-start = ((), (), s32[]{:S(2)}) async-start(), calls=%async_computation | async-start | bytes 4866048 | tf_op jit(solution)/shard_map/psum | solution.py:157
  7.9 22.3 %collective-permute-start.7 = (bf16[1,1,4,128]{3,2,1,0:T(4,128)(2,1)S(1)}, bf16[1,1,4,128]{3,2,1,0:T(4,128)(2,1)S(1)}, u32[]{:S(2)}, u32[]{:S(2)}) collective-permute-start(bf16[1,1,4,128]{3,2,1,0:T(4,128)(2,1)S(1)} %get-tuple-element.74), channel_id=1, source_target_pairs={{4,0},{8,4},{12,8},{16,12},{20,16},{24,20},{28,24},{32,28},{36,32}... | collective-permute-start | bytes 3080 | tf_op jit(solution)/shard_map/ppermute | solution.py:15
  13.1 17.1 %collective-permute-start.6 = (bf16[1,1,4,128]{3,2,1,0:T(4,128)(2,1)S(1)}, bf16[1,1,4,128]{3,2,1,0:T(4,128)(2,1)S(1)}, u32[]{:S(2)}, u32[]{:S(2)}) collective-permute-start(bf16[1,1,4,128]{3,2,1,0:T(4,128)(2,1)S(1)} %get-tuple-element.73), channel_id=1, source_target_pairs={{0,4},{4,8},{8,12},{12,16},{16,20},{20,24},{24,28},{28,32},{32,36}... | collective-permute-start | bytes 3080 | tf_op jit(solution)/shard_map/ppermute | solution.py:14
  15.0 10.1 %collective-permute-start.3 = (bf16[1,1,4,128]{3,2,1,0:T(4,128)(2,1)S(1)}, bf16[1,1,4,128]{3,2,1,0:T(4,128)(2,1)S(1)}, u32[]{:S(2)}, u32[]{:S(2)}) collective-permute-start(bf16[1,1,4,128]{3,2,1,0:T(4,128)(2,1)S(1)} %get-tuple-element.72), channel_id=1, source_target_pairs={{4,0},{8,4},{12,8},{16,12},{20,16},{24,20},{28,24},{32,28},{36,32}... | collective-permute-start | bytes 3080 | tf_op jit(solution)/shard_map/ppermute | solution.py:15
  17.4 11.3 %collective-permute-start.2 = (bf16[1,1,4,128]{3,2,1,0:T(4,128)(2,1)S(1)}, bf16[1,1,4,128]{3,2,1,0:T(4,128)(2,1)S(1)}, u32[]{:S(2)}, u32[]{:S(2)}) collective-permute-start(bf16[1,1,4,128]{3,2,1,0:T(4,128)(2,1)S(1)} %get-tuple-element.71), channel_id=1, source_target_pairs={{0,4},{4,8},{8,12},{12,16},{16,20},{20,24},{24,28},{28,32},{32,36}... | collective-permute-start | bytes 3080 | tf_op jit(solution)/shard_map/ppermute | solution.py:14
  21.4 9.2 %collective-permute-start.1 = (bf16[1,1,128,128]{3,2,1,0:T(8,128)(2,1)S(1)}, bf16[1,1,128,128]{3,2,1,0:T(8,128)(2,1)S(1)}, u32[]{:S(2)}, u32[]{:S(2)}) collective-permute-start(bf16[1,1,128,128]{3,2,1,0:T(8,128)(2,1)S(1)} %get-tuple-element.68), channel_id=1, source_target_pairs={{4,0},{8,4},{12,8},{16,12},{20,16},{24,20},{28,24},{32,28},{36,32}... | collective-permute-start | bytes 98312 | tf_op jit(solution)/shard_map/ppermute | solution.py:15
  24.4 6.2 %copy-start.1 = (bf16[1,4,128,128]{3,2,1,0:T(8,128)(2,1)S(1)}, bf16[1,4,128,128]{3,2,1,0:T(8,128)(2,1)}, u32[]{:S(2)}) copy-start(bf16[1,4,128,128]{3,2,1,0:T(8,128)(2,1)} %param.9) | copy-start | bytes 393220
  25.1 5.5 %collective-permute-start = (bf16[1,1,128,128]{3,2,1,0:T(8,128)(2,1)S(1)}, bf16[1,1,128,128]{3,2,1,0:T(8,128)(2,1)S(1)}, u32[]{:S(2)}, u32[]{:S(2)}) collective-permute-start(bf16[1,1,128,128]{3,2,1,0:T(8,128)(2,1)S(1)} %get-tuple-element.67), channel_id=1, source_target_pairs={{0,4},{4,8},{8,12},{12,16},{16,20},{20,24},{24,28},{28,32},{32,36}... | collective-permute-start | bytes 98312 | tf_op jit(solution)/shard_map/ppermute | solution.py:14
  30.2 1.3 copy-start
  30.2 1.3 copy-start.5
  36.2 1.0 copy-start.2
  37.5 5.9 %collective-permute-start.5 = (bf16[1,1,128,128]{3,2,1,0:T(8,128)(2,1)S(1)}, bf16[1,1,128,128]{3,2,1,0:T(8,128)(2,1)S(1)}, u32[]{:S(2)}, u32[]{:S(2)}) collective-permute-start(bf16[1,1,128,128]{3,2,1,0:T(8,128)(2,1)S(1)} %get-tuple-element.64), channel_id=1, source_target_pairs={{4,0},{8,4},{12,8},{16,12},{20,16},{24,20},{28,24},{32,28},{36,32}... | collective-permute-start | bytes 98312 | tf_op jit(solution)/shard_map/ppermute | solution.py:15
  39.4 4.7 %collective-permute-start.4 = (bf16[1,1,128,128]{3,2,1,0:T(8,128)(2,1)S(1)}, bf16[1,1,128,128]{3,2,1,0:T(8,128)(2,1)S(1)}, u32[]{:S(2)}, u32[]{:S(2)}) collective-permute-start(bf16[1,1,128,128]{3,2,1,0:T(8,128)(2,1)S(1)} %get-tuple-element.63), channel_id=1, source_target_pairs={{0,4},{4,8},{8,12},{12,16},{16,20},{20,24},{24,28},{28,32},{32,36}... | collective-permute-start | bytes 98312 | tf_op jit(solution)/shard_map/ppermute | solution.py:14
  51.5 10.1 %collective-permute-start.9 = (bf16[1,1,128,512]{3,2,1,0:T(8,128)(2,1)S(1)}, bf16[1,1,128,512]{3,2,1,0:T(8,128)(2,1)S(1)}, u32[]{:S(2)}, u32[]{:S(2)}) collective-permute-start(bf16[1,1,128,512]{3,2,1,0:T(8,128)(2,1)S(1)} %get-tuple-element.46), channel_id=1, source_target_pairs={{4,0},{8,4},{12,8},{16,12},{20,16},{24,20},{28,24},{32,28},{36,32}... | collective-permute-start | bytes 393224 | tf_op jit(solution)/shard_map/ppermute | solution.py:15
  53.5 8.2 %collective-permute-start.8 = (bf16[1,1,128,512]{3,2,1,0:T(8,128)(2,1)S(1)}, bf16[1,1,128,512]{3,2,1,0:T(8,128)(2,1)S(1)}, u32[]{:S(2)}, u32[]{:S(2)}) collective-permute-start(bf16[1,1,128,512]{3,2,1,0:T(8,128)(2,1)S(1)} %get-tuple-element.45), channel_id=1, source_target_pairs={{0,4},{4,8},{8,12},{12,16},{16,20},{20,24},{24,28},{28,32},{32,36}... | collective-permute-start | bytes 393224 | tf_op jit(solution)/shard_map/ppermute | solution.py:14
  66.1 109.8 %collective-permute-start.11 = (bf16[1,1,128,512]{3,2,1,0:T(8,128)(2,1)S(1)}, bf16[1,1,128,512]{3,2,1,0:T(8,128)(2,1)S(1)}, u32[]{:S(2)}, u32[]{:S(2)}) collective-permute-start(bf16[1,1,128,512]{3,2,1,0:T(8,128)(2,1)S(1)} %get-tuple-element.42), channel_id=1, source_target_pairs={{4,0},{8,4},{12,8},{16,12},{20,16},{24,20},{28,24},{32,28},{36,32}... | collective-permute-start | bytes 393224 | tf_op jit(solution)/shard_map/ppermute | solution.py:15
  68.1 107.9 %collective-permute-start.10 = (bf16[1,1,128,512]{3,2,1,0:T(8,128)(2,1)S(1)}, bf16[1,1,128,512]{3,2,1,0:T(8,128)(2,1)S(1)}, u32[]{:S(2)}, u32[]{:S(2)}) collective-permute-start(bf16[1,1,128,512]{3,2,1,0:T(8,128)(2,1)S(1)} %get-tuple-element.41), channel_id=1, source_target_pairs={{0,4},{4,8},{8,12},{12,16},{16,20},{20,24},{24,28},{28,32},{32,36}... | collective-permute-start | bytes 393224 | tf_op jit(solution)/shard_map/ppermute | solution.py:14
  358.8 3.3 copy-start.4
Sparse Core Ops, SparseCore 0:
  78.3 280.4 all-reduce.8
where the time goes:
time: 372 us; the launch traced here: 370 us
  waiting for transfers between devices  179 us (48%)
  blocking collectives  97.8 us (26%)
  starting transfers between devices  35.7 us (10%)
  matrix products  27.3 us (7%)
  between operations  14.8 us (4%)
  local copies, waits for them, and re-layouts  8.44 us (2%)
  other arithmetic  6.27 us (2%)
    psum x1, waiting for transfers between devices, on_device(): lax.psum((grad_w_hidden, grad_w_rain, grad_bias), ('space', 'event'))  179 us
    psum x1, blocking collectives, on_device(): lax.psum((grad_w_hidden, grad_w_rain, grad_bias), ('space', 'event'))  97.8 us
    ppermute x6, starting transfers between devices, with_halo(): before = lax.ppermute(last, axis, up)  20.4 us
    ppermute x6, starting transfers between devices, with_halo(): after = lax.ppermute(first, axis, down)  15.2 us
    dot_general x18, matrix products, forward_gates(): jnp.dot(rain_taps, rain_weight[tap], preferred_element_type=jnp.float32)  7.72 us
  transfers between devices with their start and end apart: 13, of which 2 were waited for; matrix products, arithmetic and copies ran while one was open for 5% of the time, Pallas kernels for 0%

commit v1 on v0

v1 whole, which is shorter than its diff:
```python
import functools

import jax
import jax.numpy as jnp
from jax import lax
from jax.experimental import pallas as pl
from jax.experimental.pallas import tpu as pltpu
from jax.sharding import PartitionSpec as P

F32 = jnp.float32
BF16 = jnp.bfloat16
NN = (((1,), (0,)), ((), ()))
NT = (((1,), (1,)), ((), ()))
TN = (((0,), (0,)), ((), ()))
SMEM = pl.BlockSpec(memory_space=pltpu.SMEM)
VMEM = pl.BlockSpec(memory_space=pltpu.VMEM)
LINES = 1216


def dot(a, b, dims):
    return lax.dot_general(a, b, dims, preferred_element_type=F32)


def call(body, n_in, outs, scratch=(), aliases=None):
    return pl.pallas_call(
        body,
        in_specs=[SMEM] + [VMEM] * n_in,
        out_specs=[VMEM] * len(outs),
        out_shape=[jax.ShapeDtypeStruct(shape, dtype) for shape, dtype in outs],
        scratch_shapes=[pltpu.VMEM(shape, dtype) for shape, dtype in scratch],
        input_output_aliases=aliases or {},
    )


def sigmoid(x):
    return 0.5 * jnp.tanh(0.5 * x) + 0.5


def fill_columns(rows_ref, wide_ref):
    at = lax.broadcasted_iota(jnp.int32, (128, 128), 0)
    for row in range(6):
        cells = rows_ref[row].astype(F32)
        spot = slice(row * 128, row * 128 + 128)
        before = jnp.where(at == 0, 0.0, pltpu.roll(cells, 1, 0))
        after = jnp.where(at == 127, 0.0, pltpu.roll(cells, 127, 0))
        wide_ref[spot, 0:128] = before.astype(BF16)
        wide_ref[spot, 128:256] = rows_ref[row]
        wide_ref[spot, 256:384] = after.astype(BF16)


def fold_columns(wide):
    at = lax.broadcasted_iota(jnp.int32, (128, 128), 0)
    before = jnp.where(at == 127, 0.0, pltpu.roll(wide[:, 0:128], 127, 0))
    after = jnp.where(at == 0, 0.0, pltpu.roll(wide[:, 256:384], 1, 0))
    return before + wide[:, 128:256] + after


def fill_rain(rows_ref, taps_ref):
    at = lax.broadcasted_iota(jnp.int32, (24, 128), 1)
    rows = rows_ref[...]
    shifted = (
        jnp.where(at == 0, 0.0, pltpu.roll(rows, 1, 1)),
        rows,
        jnp.where(at == 127, 0.0, pltpu.roll(rows, 127, 1)),
    )
    for row in range(4):
        for row_off in range(3):
            for col_off in range(3):
                tap = 3 * row_off + col_off
                first = (row + row_off) * 4
                taps_ref[tap * 4 : tap * 4 + 4, row * 128 : row * 128 + 128] = shifted[col_off][
                    first : first + 4
                ]
    line = lax.broadcasted_iota(jnp.int32, (28, 512), 0)
    taps_ref[36:64, :] = jnp.where(line == 0, 1.0, 0.0)


def add_up_gates(wide_ref, rain_taps, weight_ref, rain_weight_ref, bias_ref, sums_ref):
    sums_ref[...] = dot(wide_ref[0:512, :], weight_ref[0], NN)
    sums_ref[...] += dot(wide_ref[128:640, :], weight_ref[1], NN)
    sums_ref[...] += dot(wide_ref[256:768, :], weight_ref[2], NN)
    sums_ref[...] += dot(rain_taps, rain_weight_ref[...], TN) + bias_ref[...]


def border_kernel(side_ref, hidden_ref, rain_ref, to_a_ref, to_b_ref):
    side = side_ref[0]
    for out_ref, row in ((to_a_ref, 3 * (1 - side)), (to_b_ref, 3 * side)):
        out_ref[0:128, :] = hidden_ref[row]
        rows = jnp.concatenate(
            [rain_ref[0, row].astype(F32), rain_ref[1, row].astype(F32)], axis=0
        )
        out_ref[128:136, :] = rows.astype(BF16)


def first_kernel(
    side_ref, hidden_ref, from_a_ref, from_b_ref, rain_ref, weight_ref, rain_weight_ref, bias_ref,
    cell_ref, land_ref,
    new_ref, to_a_ref, to_b_ref, cell_new_ref, gates_ref, mask_ref, taps0_ref, taps1_ref, wide_ref,
    rows_ref, rain_rows_ref, taps_ref, sums_ref,
):
    side = side_ref[0]
    rows_ref[1:5] = hidden_ref[...]
    rows_ref[5 * (1 - side)] = from_a_ref[0:128, :]
    rows_ref[5 * side] = from_b_ref[0:128, :]
    fill_columns(rows_ref, wide_ref)
    halo_a = from_a_ref[128:136, :].astype(F32)
    halo_b = from_b_ref[128:136, :].astype(F32)
    top = jnp.where(side == 0, halo_b, halo_a)
    bottom = jnp.where(side == 0, halo_a, halo_b)
    for step, out_ref in ((0, taps0_ref), (1, taps1_ref)):
        rain_rows_ref[0:4, :] = top[4 * step : 4 * step + 4]
        for row in range(4):
            rain_rows_ref[4 * row + 4 : 4 * row + 8, :] = rain_ref[step, row].astype(F32)
        rain_rows_ref[20:24, :] = bottom[4 * step : 4 * step + 4]
        fill_rain(rain_rows_ref, taps_ref)
        out_ref[...] = taps_ref[...].astype(BF16)
    land = land_ref[...].astype(F32)
    for row in range(4):
        spread = jnp.broadcast_to(land[row : row + 1, :], (128, 128))
        mask_ref[row * 128 : row * 128 + 128, :] = jnp.transpose(spread)
    add_up_gates(wide_ref, taps0_ref[...], weight_ref, rain_weight_ref, bias_ref, sums_ref)
    for row in range(4):
        spot = slice(row * 128, row * 128 + 128)
        enter = sigmoid(sums_ref[spot, 0:128])
        forget = sigmoid(sums_ref[spot, 128:256])
        leave = sigmoid(sums_ref[spot, 256:384])
        update = jnp.tanh(sums_ref[spot, 384:512])
        gates_ref[spot, 0:128] = enter
        gates_ref[spot, 128:256] = forget
        gates_ref[spot, 256:384] = leave
        gates_ref[spot, 384:512] = update
        cell_new = forget * cell_ref[spot, :] + enter * update
        cell_new_ref[spot, :] = cell_new
        new_ref[row] = (mask_ref[spot, :] * leave * jnp.tanh(cell_new)).astype(BF16)
    to_a_ref[...] = new_ref[3 * (1 - side)]
    to_b_ref[...] = new_ref[3 * side]


def gate_gradients(gates, cell_prev, cell_new, mask, grad_hidden, grad_cell):
    enter, forget, leave, update = gates
    squash = jnp.tanh(cell_new)
    masked = grad_hidden * mask
    grad_cell = grad_cell + masked * leave * (1.0 - squash * squash)
    return (
        (
            grad_cell * update * enter * (1.0 - enter),
            grad_cell * cell_prev * forget * (1.0 - forget),
            masked * squash * leave * (1.0 - leave),
            grad_cell * enter * (1.0 - update * update),
        ),
        grad_cell * forget,
    )


def send_borders(side, grad_ref, weight_ref, edges_ref, to_a_ref, to_b_ref):
    edges_ref[0] = fold_columns(dot(grad_ref[0:128, :], weight_ref[0], NT))
    edges_ref[1] = fold_columns(dot(grad_ref[384:512, :], weight_ref[2], NT))
    to_a_ref[...] = edges_ref[1 - side]
    to_b_ref[...] = edges_ref[side]


def second_kernel(
    side_ref, hidden_ref, from_a_ref, from_b_ref, taps_ref, weight_ref, rain_weight_ref, bias_ref,
    cell_ref, mask_ref, cotangent_ref,
    new_ref, grad_ref, grad_cell_ref, to_a_ref, to_b_ref, wide_ref,
    rows_ref, sums_ref, edges_ref,
):
    side = side_ref[0]
    rows_ref[1:5] = hidden_ref[...]
    rows_ref[5 * (1 - side)] = from_a_ref[...]
    rows_ref[5 * side] = from_b_ref[...]
    fill_columns(rows_ref, wide_ref)
    add_up_gates(wide_ref, taps_ref[...], weight_ref, rain_weight_ref, bias_ref, sums_ref)
    for row in range(4):
        spot = slice(row * 128, row * 128 + 128)
        enter = sigmoid(sums_ref[spot, 0:128])
        forget = sigmoid(sums_ref[spot, 128:256])
        leave = sigmoid(sums_ref[spot, 256:384])
        update = jnp.tanh(sums_ref[spot, 384:512])
        mask = mask_ref[spot, :]
        cell = cell_ref[spot, :]
        cell_new = forget * cell + enter * update
        new_ref[row] = (mask * leave * jnp.tanh(cell_new)).astype(BF16)
        parts, grad_cell = gate_gradients(
            (enter, forget, leave, update), cell, cell_new, mask, cotangent_ref[row], 0.0
        )
        grad_cell_ref[spot, :] = grad_cell
        for part in range(4):
            grad_ref[spot, part * 128 : part * 128 + 128] = parts[part].astype(BF16)
    send_borders(side, grad_ref, weight_ref, edges_ref, to_a_ref, to_b_ref)


def spread_rows(grad_ref, weight_ref, wide_sum_ref):
    wide_sum_ref[...] = dot(grad_ref[...], weight_ref[1], NT)
    wide_sum_ref[0:384, :] += dot(grad_ref[128:512, :], weight_ref[0], NT)
    wide_sum_ref[128:512, :] += dot(grad_ref[0:384, :], weight_ref[2], NT)


def weight_gradients(side, wide_ref, taps_ref, grad_ref, outs, carried):
    for out, (out_ref, old_ref) in enumerate(zip(outs, carried)):
        start = pl.multiple_of((side if out == 0 else 1 - side) * 256, 256)
        grad = grad_ref[:, pl.ds(start, 256)]
        for row_off in range(3):
            total = dot(wide_ref[row_off * 128 : row_off * 128 + 512, :], grad, TN)
            spot = slice(row_off * 384, row_off * 384 + 384)
            for part in range(2):
                piece = total[:, part * 128 : part * 128 + 128]
                if old_ref is not None:
                    piece = piece + old_ref[part, spot, :]
                out_ref[part, spot, :] = piece
        total = dot(taps_ref[...], grad, NN)
        for part in range(2):
            piece = total[:, part * 128 : part * 128 + 128]
            if old_ref is not None:
                piece = piece + old_ref[part, 1152:1216, :]
            out_ref[part, 1152:1216, :] = piece


def third_kernel(
    side_ref, grad_ref, weight_ref, wide_ref, taps_ref,
    kept_ref, given_ref, own_ref,
    wide_sum_ref,
):
    spread_rows(grad_ref, weight_ref, wide_sum_ref)
    for row in range(4):
        own_ref[row] = fold_columns(wide_sum_ref[row * 128 : row * 128 + 128, :])
    weight_gradients(
        side_ref[0], wide_ref, taps_ref, grad_ref, (kept_ref, given_ref), (None, None)
    )


def fourth_kernel(
    side_ref, old_kept_ref, old_given_ref, own_ref, from_a_ref, from_b_ref, cotangent_ref,
    gates_ref, cell_ref, cell_new_ref, mask_ref, grad_cell_ref, weight_ref, wide_ref, taps_ref,
    kept_ref, given_ref, grad_ref, to_a_ref, to_b_ref,
    total_ref, edges_ref,
):
    side = side_ref[0]
    total_ref[...] = own_ref[...] + cotangent_ref[...]
    total_ref[3 * (1 - side)] += from_a_ref[...]
    total_ref[3 * side] += from_b_ref[...]
    for row in range(4):
        spot = slice(row * 128, row * 128 + 128)
        gates = [gates_ref[spot, part * 128 : part * 128 + 128] for part in range(4)]
        parts, _ = gate_gradients(
            gates, cell_ref[spot, :], cell_new_ref[spot, :], mask_ref[spot, :], total_ref[row],
            grad_cell_ref[spot, :],
        )
        for part in range(4):
            grad_ref[spot, part * 128 : part * 128 + 128] = parts[part].astype(BF16)
    weight_gradients(
        side, wide_ref, taps_ref, grad_ref, (kept_ref, given_ref), (old_kept_ref, old_given_ref)
    )
    send_borders(side, grad_ref, weight_ref, edges_ref, to_a_ref, to_b_ref)


def last_kernel(
    side_ref, grad_ref, weight_ref, from_a_ref, from_b_ref, out_ref, wide_sum_ref
):
    side = side_ref[0]
    spread_rows(grad_ref, weight_ref, wide_sum_ref)
    for row in range(4):
        out_ref[row] = fold_columns(wide_sum_ref[row * 128 : row * 128 + 128, :])
    out_ref[3 * (1 - side)] += from_a_ref[...]
    out_ref[3 * side] += from_b_ref[...]


def pair_kernel(side_ref, kept_ref, got_ref, out_ref):
    for part in range(2):
        for piece in range(8):
            spot = slice(piece * 152, piece * 152 + 152)
            out_ref[part * 8 + piece] = (kept_ref[part, spot, :] + got_ref[part, spot, :]).astype(
                BF16
            )


def fold_kernel(side_ref, parts_ref, out_ref):
    total = parts_ref[0].astype(F32)
    for part in range(1, parts_ref.shape[0]):
        total = total + parts_ref[part].astype(F32)
    total = total.astype(BF16)
    for part in range(out_ref.shape[0]):
        out_ref[part] = total


def unpack_kernel(side_ref, mine_ref, other_ref, hidden_ref, rain_ref, bias_ref):
    for half, source_ref in ((side_ref[0], mine_ref), (1 - side_ref[0], other_ref)):
        for part in range(2):
            lanes = pl.ds(pl.multiple_of(half * 256 + part * 128, 128), 128)
            hidden_ref[:, lanes] = source_ref[part, 0:1152, :].astype(F32)
            tail = source_ref[part, 1152:1216, :].astype(F32)
            rain_ref[:, lanes] = tail[0:36]
            bias_ref[:, lanes] = tail[36:37]


def device_groups(deep, wide, across):
    planes = [
        [((z * wide + y) * 2 + core) * across + x for y in range(wide) for x in range(across)]
        for z in range(deep)
        for core in range(2)
    ]
    columns = [[z * wide * 2 + low for z in range(deep)] for low in range(wide * 2)]
    return (planes, columns)


def sum_everywhere(side, kept, given, swap):
    planes, columns = device_groups(8, 4, 4)
    fold = lambda parts, copies: call(fold_kernel, 1, [((copies, 152, 128), BF16)])(side, parts)[0]
    parts = call(pair_kernel, 2, [((16, 152, 128), BF16)])(side, kept, swap(given))[0]
    parts = lax.all_to_all(parts, ("space", "event"), 0, 0, axis_index_groups=planes)
    parts = lax.all_to_all(fold(parts, 8), "space", 0, 0, axis_index_groups=columns)
    parts = lax.all_to_all(fold(parts, 16), ("space", "event"), 0, 0, axis_index_groups=planes)
    mine = parts.reshape(2, LINES, 128)
    return call(
        unpack_kernel, 2, [((1152, 512), F32), ((36, 512), F32), ((1, 512), F32)]
    )(side, mine, swap(mine))


def on_device(
    rain, hidden_init, cell_init, land_mask, hidden_weight, rain_weight, gate_bias, cotangent
):
    size = lax.axis_size("space")
    side = lax.rem(lax.axis_index("space"), 2).astype(jnp.int32)[None]
    near = [(i, i ^ 1) for i in range(size)]
    far = [(i, i + 1) for i in range(1, size - 1, 2)] + [(i + 1, i) for i in range(1, size - 1, 2)]
    swap = lambda x: lax.ppermute(x, "space", near)
    across = lambda x: lax.ppermute(x, "space", far)
    weight = hidden_weight.reshape(3, 384, 512)
    rain_lines = jnp.pad(rain_weight.reshape(36, 512), ((0, 28), (0, 0)))
    bias = gate_bias.reshape(1, 512)
    hidden = hidden_init[0]
    rain = rain[0]
    cell = cell_init.reshape(512, 128)
    row = ((128, 128), F32)

    to_a, to_b = call(border_kernel, 2, [((136, 128), BF16)] * 2)(side, hidden, rain)
    new, to_a, to_b, cell_new, gates, mask, taps0, taps1, wide0 = call(
        first_kernel,
        9,
        [
            ((4, 128, 128), BF16), ((128, 128), BF16), ((128, 128), BF16), ((512, 128), F32),
            ((512, 512), F32), ((512, 128), F32), ((64, 512), BF16), ((64, 512), BF16),
            ((768, 384), BF16),
        ],
        [((6, 128, 128), BF16), ((24, 128), F32), ((64, 512), F32), ((512, 512), F32)],
    )(side, hidden, swap(to_a), across(to_b), rain, weight, rain_lines, bias, cell, land_mask)
    final, grad1, grad_cell, to_a, to_b, wide1 = call(
        second_kernel,
        10,
        [
            ((4, 128, 128), BF16), ((512, 512), BF16), ((512, 128), F32), row, row,
            ((768, 384), BF16),
        ],
        [((6, 128, 128), BF16), ((512, 512), F32), ((2, 128, 128), F32)],
    )(
        side, new, swap(to_a), across(to_b), taps1, weight, rain_lines, bias, cell_new, mask,
        cotangent[0, 1],
    )
    from_a, from_b = (swap(to_a), across(to_b))
    pile = ((2, LINES, 128), F32)
    kept, given, own = call(
        third_kernel, 4, [pile, pile, ((4, 128, 128), F32)], [((512, 384), F32)]
    )(side, grad1, weight, wide1, taps1)
    kept, given, grad0, to_a, to_b = call(
        fourth_kernel,
        14,
        [pile, pile, ((512, 512), BF16), row, row],
        [((4, 128, 128), F32), ((2, 128, 128), F32)],
        {1: 0, 2: 1},
    )(
        side, kept, given, own, from_a, from_b, cotangent[0, 0], gates, cell, cell_new, mask,
        grad_cell, weight, wide0, taps0,
    )
    grad_hidden = call(last_kernel, 4, [((4, 128, 128), F32)], [((512, 384), F32)])(
        side, grad0, weight, swap(to_a), across(to_b)
    )[0]
    grad_w_hidden, grad_w_rain, grad_bias = sum_everywhere(side, kept, given, swap)
    return (
        final[None],
        grad_hidden[None],
        grad_w_hidden.reshape(hidden_weight.shape),
        grad_w_rain.reshape(rain_weight.shape),
        grad_bias.reshape(gate_bias.shape),
    )


def solution(mesh):
    in_specs = (
        P("event", None, "space", None, None),
        P("event", "space", None, None),
        P("event", "space", None, None),
        P("space", None),
        P(),
        P(),
        P(),
        P("event", None, "space", None, None),
    )
    out_specs = (P("event", "space", None, None), P("event", "space", None, None), P(), P(), P())
    return jax.shard_map(
        on_device, mesh=mesh, in_specs=in_specs, out_specs=out_specs, check_vma=False
    )
```

time: 372 us -> 126 us (0.34)
  waiting for transfers between devices: 179 us -> 11.1 us
  blocking collectives: 97.8 us -> 55.5 us
  Pallas kernels: 0 us -> 32.6 us
  matrix products: 27.3 us -> 0 us
  starting transfers between devices: 35.7 us -> 16.5 us
  between operations: 14.8 us -> 0.76 us
  other arithmetic: 6.27 us -> 0 us
    psum x1 -> x0, waiting for transfers between devices: 179 us -> none  [on_device(): lax.psum((grad_w_hidden, grad_w_rain, grad_bias), ('space', 'event'))]
    psum x1 -> x0, blocking collectives: 97.8 us -> none  [on_device(): lax.psum((grad_w_hidden, grad_w_rain, grad_bias), ('space', 'event'))]
    all_to_all x0 -> x3, blocking collectives: none -> 55.5 us  [the longest x1 22.4 us: sum_everywhere(): lax.all_to_all(parts, ('space', 'event'), 0, 0, axis_index_groups=planes)]
    pallas_call x0 -> x10, Pallas kernels: none -> 32.6 us  [the longest x1 5.9 us: on_device(): call(fourth_kernel, 14, [pile, pile, ((512, 512), BF16), row, row], [((4,...]
    dot_general x90 -> x0, matrix products: 27.3 us -> none  [the longest x18 7.72 us: forward_gates(): jnp.dot(rain_taps, rain_weight[tap], preferred_element_type=jnp.float32)]
    ppermute x12 -> x10, starting transfers between devices: 35.6 us -> 16.5 us  [the longest x4 8.72 us: on_device(): across = lambda x: lax.ppermute(x, 'space', far)]
    ppermute x12 -> x10, waiting for transfers between devices: 0.67 us -> 11.1 us  [the longest x4 7.91 us: on_device(): across = lambda x: lax.ppermute(x, 'space', far)]
  transfers between devices with their start and end apart: 13 -> 10, of which waited for: 2 -> 4; matrix products, arithmetic and copies ran while one was open for 5% -> 2% of each run, Pallas kernels for 0% -> 6%
where the time goes in v1:
time: 126 us; the launch traced here: 125 us
  blocking collectives  55.5 us (44%)
  Pallas kernels  32.6 us (26%)
  starting transfers between devices  16.5 us (13%)
  waiting for transfers between devices  11.1 us (9%)
  local copies, waits for them, and re-layouts  8.21 us (7%)
    all_to_all x1, blocking collectives, sum_everywhere(): lax.all_to_all(parts, ('space', 'event'), 0, 0, axis_index_groups=planes)  22.4 us
    all_to_all x1, blocking collectives, sum_everywhere(): lax.all_to_all(fold(parts, 8), 'space', 0, 0, axis_index_groups=columns)  19.9 us
    all_to_all x1, blocking collectives, sum_everywhere(): lax.all_to_all(fold(parts, 16), ('space', 'event'), 0, 0, axis_index_grou...  13.1 us
    ppermute x4, starting transfers between devices, on_device(): across = lambda x: lax.ppermute(x, 'space', far)  8.72 us
    ppermute x4, waiting for transfers between devices, on_device(): across = lambda x: lax.ppermute(x, 'space', far)  7.91 us
    ppermute x6, starting transfers between devices, on_device(): swap = lambda x: lax.ppermute(x, 'space', near)  7.82 us
    pallas_call x1, Pallas kernels, on_device(): call(fourth_kernel, 14, [pile, pile, ((512, 512), BF16), row, row], [((4,...  5.9 us
    unnamed x28, local copies, waits for them, and re-layouts  4.42 us
  transfers between devices with their start and end apart: 10, of which 4 were waited for; matrix products, arithmetic and copies ran while one was open for 2% of the time, Pallas kernels for 6%

profile of v1, /device:TPU:1, one launch (start us, length us, event | category | flops | bytes accessed | tf_op | source)
XLA Modules:
  0.0 124.7 jit_solution(10699983533254099824)
XLA Ops:
  0.6 1.6 %shard_map.119 = (bf16[136,128]{1,0:T(8,128)(2,1)}, bf16[136,128]{1,0:T(8,128)(2,1)}) custom-call(s32[1]{0:T(128)} %bitcast.side_ref, bf16[4,128,128]{2,1,0:T(8,128)(2,1)} %bitcast.24, bf16[2,4,4,128]{3,2,1,0:T(4,128)(2,1)} %bitcast.27), custom_call_target="tpu_custom_call" | custom-call | tf_op jit(solution)/shard_map/pallas_call | solution.py:336
  2.2 3.2 %collective-permute-start = (bf16[136,128]{1,0:T(8,128)(2,1)}, bf16[136,128]{1,0:T(8,128)(2,1)S(1)}, u32[]{:S(2)}, u32[]{:S(2)}) collective-permute-start(bf16[136,128]{1,0:T(8,128)(2,1)} %get-tuple-element.33), channel_id=1, source_target_pairs={{0,4},{4,0},{8,12},{12,8},{16,20},{20,16},{24,28},{28,24},{32,36},... | collective-permute-start | bytes 104456 | tf_op jit(solution)/shard_map/ppermute | solution.py:326
  5.5 1.9 %collective-permute-start.1 = (bf16[136,128]{1,0:T(8,128)(2,1)}, bf16[136,128]{1,0:T(8,128)(2,1)S(1)}, u32[]{:S(2)}, u32[]{:S(2)}) collective-permute-start(bf16[136,128]{1,0:T(8,128)(2,1)} %get-tuple-element.34), channel_id=1, source_target_pairs={{4,8},{12,16},{20,24},{28,32},{36,40},{44,48},{52,56},{60,64},{68,... | collective-permute-start | bytes 104456 | tf_op jit(solution)/shard_map/ppermute | solution.py:327
  8.8 2.1 %collective-permute-done.1.from_b_ref = bf16[136,128]{1,0:T(8,128)(2,1)S(1)} collective-permute-done((bf16[136,128]{1,0:T(8,128)(2,1)}, bf16[136,128]{1,0:T(8,128)(2,1)S(1)}, u32[]{:S(2)}, u32[]{:S(2)}) %collective-permute-start.1) | collective-permute-done | bytes 34848 | tf_op jit(solution)/shard_map/ppermute | solution.py:327
  11.6 4.0 %shard_map.120 = (bf16[4,128,128]{2,1,0:T(8,128)(2,1)}, bf16[128,128]{1,0:T(8,128)(2,1)}, bf16[128,128]{1,0:T(8,128)(2,1)}, f32[512,128]{1,0:T(8,128)}, f32[512,...) custom-call(s32[1]{0:T(128)} %bitcast.side_ref, ...), custom_call_target="tpu_custom_call" | custom-call | tf_op jit(solution)/shard_map/pallas_call | solution.py:337
  15.7 2.0 %collective-permute-start.3 = (bf16[128,128]{1,0:T(8,128)(2,1)}, bf16[128,128]{1,0:T(8,128)(2,1)S(1)}, u32[]{:S(2)}, u32[]{:S(2)}) collective-permute-start(bf16[128,128]{1,0:T(8,128)(2,1)} %get-tuple-element.37), channel_id=1, source_target_pairs={{4,8},{12,16},{20,24},{28,32},{36,40},{44,48},{52,56},{60,64},{68,... | collective-permute-start | bytes 98312 | tf_op jit(solution)/shard_map/ppermute | solution.py:327
  18.5 2.6 %collective-permute-done.3.from_b_ref = bf16[128,128]{1,0:T(8,128)(2,1)S(1)} collective-permute-done((bf16[128,128]{1,0:T(8,128)(2,1)}, bf16[128,128]{1,0:T(8,128)(2,1)S(1)}, u32[]{:S(2)}, u32[]{:S(2)}) %collective-permute-start.3) | collective-permute-done | bytes 32800 | tf_op jit(solution)/shard_map/ppermute | solution.py:327
  21.7 4.3 %shard_map.121 = (bf16[4,128,128]{2,1,0:T(8,128)(2,1)}, bf16[512,512]{1,0:T(8,128)(2,1)}, f32[512,128]{1,0:T(8,128)}, f32[128,128]{1,0:T(8,128)}, f32[128,128]{1,0:T(8,128)}, /*index=5*/bf16[768,384]{1,0:T(8,128)(2,1)}) custom-call(s32[1]{0:T(128)} %bitcast.side_ref, bf16[4,128,128]{2,1,0:T(8,128)(2,1)} %get-tuple-element.35.hidden_ref, ...), custom_call_target="tpu_custom_call" | custom-call | tf_op jit(solution)/shard_map/pallas_call | solution.py:347
  26.0 2.5 %collective-permute-start.5 = (f32[128,128]{1,0:T(8,128)}, f32[128,128]{1,0:T(8,128)S(1)}, u32[]{:S(2)}, u32[]{:S(2)}) collective-permute-start(f32[128,128]{1,0:T(8,128)} %get-tuple-element.48), channel_id=1, source_target_pairs={{4,8},{12,16},{20,24},{28,32},{36,40},{44,48},{52,56},{60,64},{68,... | collective-permute-start | bytes 196616 | tf_op jit(solution)/shard_map/ppermute | solution.py:327
  28.5 4.4 %shard_map.122 = (f32[2,1216,128]{2,1,0:T(8,128)}, f32[2,1216,128]{2,1,0:T(8,128)}, f32[4,128,128]{2,1,0:T(8,128)}) custom-call(s32[1]{0:T(128)} %bitcast.side_ref, bf16[512,512]{1,0:T(8,128)(2,1)} %get-tuple-element.42.grad_ref, bf16[3,384,512]{2,1,0:T(8,128)(2,1)} %bitcast.17, bf16[768,384]{1,0:T(8,128)(2,1)} %get-tuple-element.43.wide_ref, ...), custom_call_target="tpu_custom_call" | custom-call | tf_op jit(solution)/shard_map/pallas_call | solution.py:361
  33.6 5.9 %shard_map.123 = (f32[2,1216,128]{2,1,0:T(8,128)}, f32[2,1216,128]{2,1,0:T(8,128)}, bf16[512,512]{1,0:T(8,128)(2,1)}, f32[128,128]{1,0:T(8,128)}, f32[128,128]{1,0:T(8,128)}) custom-call(s32[1]{0:T(128)} %bitcast.side_ref, f32[2,1216,128]{2,1,0:T(8,128)} %get-tuple-element.44.old_kept_ref, ...), custom_call_target="tpu_custom_call", output_to_operand_aliasing={{0}: (1, {}), {1}: (2, {})} | custom-call | tf_op jit(solution)/shard_map/pallas_call | solution.py:364
  39.5 3.1 %collective-permute-done.8.got_ref = f32[2,1216,128]{2,1,0:T(8,128)S(1)} collective-permute-done((f32[2,1216,128]{2,1,0:T(8,128)}, f32[2,1216,128]{2,1,0:T(8,128)S(1)}, u32[]{:S(2)}, u32[]{:S(2)}) %collective-permute-start.8) | collective-permute-done | bytes 1245216 | tf_op jit(solution)/shard_map/ppermute | solution.py:326
  43.7 2.6 %shard_map.125 = bf16[16,152,128]{2,1,0:T(8,128)(2,1)} custom-call(s32[1]{0:T(128)} %bitcast.side_ref, f32[2,1216,128]{2,1,0:T(8,128)} %get-tuple-element.56.kept_ref, f32[2,1216,128]{2,1,0:T(8,128)} %copy-done.1), custom_call_target="tpu_custom_call" | custom-call | tf_op jit(solution)/shard_map/pallas_call | solution.py:309
  46.3 22.4 %all_to_all.15.parts_ref = bf16[16,152,128]{2,1,0:T(8,128)(2,1)} all-to-all(bf16[16,152,128]{2,1,0:T(8,128)(2,1)} %shard_map.125), channel_id=1, replica_groups={{0,1,2,3,8,9,10,11,16,17,18,19,24,25,26,27},{4,5,6,7,12,13,14,15,20,21,..., dimensions={0} | all-to-all | bytes 1245184 | tf_op jit(solution)/shard_map/all_to_all | solution.py:310
  68.8 1.9 %shard_map.126 = bf16[8,152,128]{2,1,0:T(8,128)(2,1)} custom-call(s32[1]{0:T(128)} %bitcast.side_ref, bf16[16,152,128]{2,1,0:T(8,128)(2,1)} %all_to_all.15.parts_ref), custom_call_target="tpu_custom_call" | custom-call | tf_op jit(solution)/shard_map/pallas_call | solution.py:308
  70.6 19.9 %all_to_all.16.parts_ref = bf16[8,152,128]{2,1,0:T(8,128)(2,1)} all-to-all(bf16[8,152,128]{2,1,0:T(8,128)(2,1)} %shard_map.126), channel_id=1, replica_groups={{0,32,64,96,128,160,192,224},{4,36,68,100,132,164,196,228},{8,40,72,104..., dimensions={0} | all-to-all | bytes 622592 | tf_op jit(solution)/shard_map/all_to_all | solution.py:311
  90.6 1.9 %shard_map.127 = bf16[16,152,128]{2,1,0:T(8,128)(2,1)} custom-call(s32[1]{0:T(128)} %bitcast.side_ref, bf16[8,152,128]{2,1,0:T(8,128)(2,1)} %all_to_all.16.parts_ref), custom_call_target="tpu_custom_call" | custom-call | tf_op jit(solution)/shard_map/pallas_call | solution.py:308
  92.5 13.1 %all_to_all.17 = bf16[16,152,128]{2,1,0:T(8,128)(2,1)S(1)} all-to-all(bf16[16,152,128]{2,1,0:T(8,128)(2,1)} %shard_map.127), channel_id=1, replica_groups={{0,1,2,3,8,9,10,11,16,17,18,19,24,25,26,27},{4,5,6,7,12,13,14,15,20,21,..., dimensions={0} | all-to-all | bytes 1245184 | tf_op jit(solution)/shard_map/all_to_all | solution.py:312
  105.6 4.4 %collective-permute-start.9 = (bf16[2,1216,128]{2,1,0:T(8,128)(2,1)S(1)}, bf16[2,1216,128]{2,1,0:T(8,128)(2,1)S(1)}, u32[]{:S(2)}, u32[]{:S(2)}) collective-permute-start(bf16[2,1216,128]{2,1,0:T(8,128)(2,1)S(1)} %bitcast.20), channel_id=1, source_target_pairs={{0,4},{4,0},{8,12},{12,8},{16,20},{20,16},{24,28},{28,24},{32,36},... | collective-permute-start | bytes 1867784 | tf_op jit(solution)/shard_map/ppermute | solution.py:326
  110.1 2.3 %collective-permute-start.7 = (f32[128,128]{1,0:T(8,128)S(1)}, f32[128,128]{1,0:T(8,128)S(1)}, u32[]{:S(2)}, u32[]{:S(2)}) collective-permute-start(f32[128,128]{1,0:T(8,128)S(1)} %copy-done.12), channel_id=1, source_target_pairs={{4,8},{12,16},{20,24},{28,32},{36,40},{44,48},{52,56},{60,64},{68,... | collective-permute-start | bytes 196616 | tf_op jit(solution)/shard_map/ppermute | solution.py:327
  112.4 3.2 %collective-permute-done.7.from_b_ref = f32[128,128]{1,0:T(8,128)S(1)} collective-permute-done((f32[128,128]{1,0:T(8,128)S(1)}, f32[128,128]{1,0:T(8,128)S(1)}, u32[]{:S(2)}, u32[]{:S(2)}) %collective-permute-start.7) | collective-permute-done | bytes 65568 | tf_op jit(solution)/shard_map/ppermute | solution.py:327
  116.3 3.0 %shard_map.124 = f32[4,128,128]{2,1,0:T(8,128)} custom-call(s32[1]{0:T(128)} %bitcast.side_ref, bf16[512,512]{1,0:T(8,128)(2,1)} %get-tuple-element.53.grad_ref, bf16[3,384,512]{2,1,0:T(8,128)(2,1)} %bitcast.19, f32[128,128]{1,0:T(8,128)} %copy-done.6, f32[128,128]{1,0:T(8,128)} %copy-done.7), custom_call_target="tpu_custom_call" | custom-call | tf_op jit(solution)/shard_map/pallas_call | solution.py:374
  120.1 3.0 %shard_map.128 = (f32[1152,512]{1,0:T(8,128)}, f32[36,512]{1,0:T(8,128)}, f32[1,512]{1,0:T(1,128)}) custom-call(s32[1]{0:T(128)} %bitcast.side_ref, bf16[2,1216,128]{2,1,0:T(8,128)(2,1)} %bitcast.21, bf16[2,1216,128]{2,1,0:T(8,128)(2,1)} %copy-done.2), custom_call_target="tpu_custom_call" | custom-call | tf_op jit(solution)/shard_map/pallas_call | solution.py:314
  123.1 1.5 %reshape.40 = f32[9,4,512]{2,1,0:T(4,128)} reshape(f32[36,512]{1,0:T(8,128)} %get-tuple-element.59) | data formatting | bytes 147456 | tf_op jit(solution)/shard_map/reshape | solution.py:382
  (41 shorter events, 6.9 us)
Async XLA Ops:
  0.6 17.1 %copy-start.3 = (f32[1,2,4,128,128]{4,3,2,1,0:T(8,128)S(1)}, f32[1,2,4,128,128]{4,3,2,1,0:T(8,128)}, u32[]{:S(2)}) copy-start(f32[1,2,4,128,128]{4,3,2,1,0:T(8,128)} %param.15) | copy-start | bytes 1572868
  2.2 6.6 %collective-permute-start = (bf16[136,128]{1,0:T(8,128)(2,1)}, bf16[136,128]{1,0:T(8,128)(2,1)S(1)}, u32[]{:S(2)}, u32[]{:S(2)}) collective-permute-start(bf16[136,128]{1,0:T(8,128)(2,1)} %get-tuple-element.33), channel_id=1, source_target_pairs={{0,4},{4,0},{8,12},{12,8},{16,20},{20,16},{24,28},{28,24},{32,36},... | collective-permute-start | bytes 104456 | tf_op jit(solution)/shard_map/ppermute | solution.py:326
  5.5 5.5 %collective-permute-start.1 = (bf16[136,128]{1,0:T(8,128)(2,1)}, bf16[136,128]{1,0:T(8,128)(2,1)S(1)}, u32[]{:S(2)}, u32[]{:S(2)}) collective-permute-start(bf16[136,128]{1,0:T(8,128)(2,1)} %get-tuple-element.34), channel_id=1, source_target_pairs={{4,8},{12,16},{20,24},{28,32},{36,40},{44,48},{52,56},{60,64},{68,... | collective-permute-start | bytes 104456 | tf_op jit(solution)/shard_map/ppermute | solution.py:327
  8.8 2.1 %copy-start.8 = (bf16[136,128]{1,0:T(8,128)(2,1)}, bf16[136,128]{1,0:T(8,128)(2,1)S(1)}, u32[]{:S(2)}) copy-start(bf16[136,128]{1,0:T(8,128)(2,1)S(1)} %collective-permute-done.from_a_ref) | copy-start | bytes 104452
  10.9 0.6 copy-start.9
  15.6 3.0 %collective-permute-start.2 = (bf16[128,128]{1,0:T(8,128)(2,1)}, bf16[128,128]{1,0:T(8,128)(2,1)S(1)}, u32[]{:S(2)}, u32[]{:S(2)}) collective-permute-start(bf16[128,128]{1,0:T(8,128)(2,1)} %get-tuple-element.36), channel_id=1, source_target_pairs={{0,4},{4,0},{8,12},{12,8},{16,20},{20,16},{24,28},{28,24},{32,36},... | collective-permute-start | bytes 98312 | tf_op jit(solution)/shard_map/ppermute | solution.py:326
  15.7 5.4 %collective-permute-start.3 = (bf16[128,128]{1,0:T(8,128)(2,1)}, bf16[128,128]{1,0:T(8,128)(2,1)S(1)}, u32[]{:S(2)}, u32[]{:S(2)}) collective-permute-start(bf16[128,128]{1,0:T(8,128)(2,1)} %get-tuple-element.37), channel_id=1, source_target_pairs={{4,8},{12,16},{20,24},{28,32},{36,40},{44,48},{52,56},{60,64},{68,... | collective-permute-start | bytes 98312 | tf_op jit(solution)/shard_map/ppermute | solution.py:327
  18.5 2.6 %copy-start.10 = (bf16[128,128]{1,0:T(8,128)(2,1)}, bf16[128,128]{1,0:T(8,128)(2,1)S(1)}, u32[]{:S(2)}) copy-start(bf16[128,128]{1,0:T(8,128)(2,1)S(1)} %collective-permute-done.2.from_a_ref) | copy-start | bytes 98308
  21.1 0.6 copy-start.11
  26.0 6.9 %collective-permute-start.4 = (f32[128,128]{1,0:T(8,128)}, f32[128,128]{1,0:T(8,128)S(1)}, u32[]{:S(2)}, u32[]{:S(2)}) collective-permute-start(f32[128,128]{1,0:T(8,128)} %get-tuple-element.47), channel_id=1, source_target_pairs={{0,4},{4,0},{8,12},{12,8},{16,20},{20,16},{24,28},{28,24},{32,36},... | collective-permute-start | bytes 196616 | tf_op jit(solution)/shard_map/ppermute | solution.py:326
  26.0 6.9 %collective-permute-start.5 = (f32[128,128]{1,0:T(8,128)}, f32[128,128]{1,0:T(8,128)S(1)}, u32[]{:S(2)}, u32[]{:S(2)}) collective-permute-start(f32[128,128]{1,0:T(8,128)} %get-tuple-element.48), channel_id=1, source_target_pairs={{4,8},{12,16},{20,24},{28,32},{36,40},{44,48},{52,56},{60,64},{68,... | collective-permute-start | bytes 196616 | tf_op jit(solution)/shard_map/ppermute | solution.py:327
  32.9 0.6 copy-start.4
  32.9 0.6 copy-start.5
  39.5 3.2 %collective-permute-start.8 = (f32[2,1216,128]{2,1,0:T(8,128)}, f32[2,1216,128]{2,1,0:T(8,128)S(1)}, u32[]{:S(2)}, u32[]{:S(2)}) collective-permute-start(f32[2,1216,128]{2,1,0:T(8,128)} %get-tuple-element.57), channel_id=1, source_target_pairs={{0,4},{4,0},{8,12},{12,8},{16,20},{20,16},{24,28},{28,24},{32,36},... | collective-permute-start | bytes 3735560 | tf_op jit(solution)/shard_map/ppermute | solution.py:326
  42.7 1.1 copy-start.1
  90.6 19.4 %copy-start.13 = (f32[128,128]{1,0:T(8,128)S(1)}, f32[128,128]{1,0:T(8,128)}, u32[]{:S(2)}) copy-start(f32[128,128]{1,0:T(8,128)} %get-tuple-element.54) | copy-start | bytes 196612
  90.6 19.5 %copy-start.12 = (f32[128,128]{1,0:T(8,128)S(1)}, f32[128,128]{1,0:T(8,128)}, u32[]{:S(2)}) copy-start(f32[128,128]{1,0:T(8,128)} %get-tuple-element.55) | copy-start | bytes 196612
  105.6 13.7 %copy-start = (bf16[16,152,128]{2,1,0:T(8,128)(2,1)}, bf16[16,152,128]{2,1,0:T(8,128)(2,1)S(1)}, u32[]{:S(2)}) copy-start(bf16[16,152,128]{2,1,0:T(8,128)(2,1)S(1)} %all_to_all.17) | copy-start | bytes 1867780
  105.6 13.7 %collective-permute-start.9 = (bf16[2,1216,128]{2,1,0:T(8,128)(2,1)S(1)}, bf16[2,1216,128]{2,1,0:T(8,128)(2,1)S(1)}, u32[]{:S(2)}, u32[]{:S(2)}) collective-permute-start(bf16[2,1216,128]{2,1,0:T(8,128)(2,1)S(1)} %bitcast.20), channel_id=1, source_target_pairs={{0,4},{4,0},{8,12},{12,8},{16,20},{20,16},{24,28},{28,24},{32,36},... | collective-permute-start | bytes 1867784 | tf_op jit(solution)/shard_map/ppermute | solution.py:326
  110.0 2.4 %collective-permute-start.6 = (f32[128,128]{1,0:T(8,128)S(1)}, f32[128,128]{1,0:T(8,128)S(1)}, u32[]{:S(2)}, u32[]{:S(2)}) collective-permute-start(f32[128,128]{1,0:T(8,128)S(1)} %copy-done.13), channel_id=1, source_target_pairs={{0,4},{4,0},{8,12},{12,8},{16,20},{20,16},{24,28},{28,24},{32,36},... | collective-permute-start | bytes 196616 | tf_op jit(solution)/shard_map/ppermute | solution.py:326
  110.1 5.6 %collective-permute-start.7 = (f32[128,128]{1,0:T(8,128)S(1)}, f32[128,128]{1,0:T(8,128)S(1)}, u32[]{:S(2)}, u32[]{:S(2)}) collective-permute-start(f32[128,128]{1,0:T(8,128)S(1)} %copy-done.12), channel_id=1, source_target_pairs={{4,8},{12,16},{20,24},{28,32},{36,40},{44,48},{52,56},{60,64},{68,... | collective-permute-start | bytes 196616 | tf_op jit(solution)/shard_map/ppermute | solution.py:327
  112.4 3.2 %copy-start.6 = (f32[128,128]{1,0:T(8,128)}, f32[128,128]{1,0:T(8,128)S(1)}, u32[]{:S(2)}) copy-start(f32[128,128]{1,0:T(8,128)S(1)} %collective-permute-done.6.from_a_ref) | copy-start | bytes 196612
  115.7 0.6 copy-start.7
  119.3 0.9 copy-start.2

commit v2 on v1

--- a/solution.py
+++ b/solution.py
@@ -289,7 +289,8 @@
             lanes = pl.ds(pl.multiple_of(half * 256 + part * 128, 128), 128)
             hidden_ref[:, lanes] = source_ref[part, 0:1152, :].astype(F32)
             tail = source_ref[part, 1152:1216, :].astype(F32)
-            rain_ref[:, lanes] = tail[0:36]
+            for tap in range(9):
+                rain_ref[tap, :, lanes] = tail[tap * 4 : tap * 4 + 4]
             bias_ref[:, lanes] = tail[36:37]
 
 
@@ -303,17 +304,19 @@
     return (planes, columns)
 
 
-def sum_everywhere(side, kept, given, swap):
+def sum_everywhere(side, kept, got, swap, beside):
     planes, columns = device_groups(8, 4, 4)
     fold = lambda parts, copies: call(fold_kernel, 1, [((copies, 152, 128), BF16)])(side, parts)[0]
-    parts = call(pair_kernel, 2, [((16, 152, 128), BF16)])(side, kept, swap(given))[0]
+    parts = call(pair_kernel, 2, [((16, 152, 128), BF16)])(side, kept, got)[0]
     parts = lax.all_to_all(parts, ("space", "event"), 0, 0, axis_index_groups=planes)
     parts = lax.all_to_all(fold(parts, 8), "space", 0, 0, axis_index_groups=columns)
     parts = lax.all_to_all(fold(parts, 16), ("space", "event"), 0, 0, axis_index_groups=planes)
     mine = parts.reshape(2, LINES, 128)
-    return call(
-        unpack_kernel, 2, [((1152, 512), F32), ((36, 512), F32), ((1, 512), F32)]
-    )(side, mine, swap(mine))
+    mine, held = lax.optimization_barrier((mine, beside[0]))
+    other, hidden = swap(mine), beside[1](held)
+    return hidden, *call(
+        unpack_kernel, 2, [((1152, 512), F32), ((9, 4, 512), F32), ((1, 512), F32)]
+    )(side, mine, other)
 
 
 def on_device(
@@ -371,15 +374,18 @@
         side, kept, given, own, from_a, from_b, cotangent[0, 0], gates, cell, cell_new, mask,
         grad_cell, weight, wide0, taps0,
     )
-    grad_hidden = call(last_kernel, 4, [((4, 128, 128), F32)], [((512, 384), F32)])(
-        side, grad0, weight, swap(to_a), across(to_b)
+    got, from_a, from_b = lax.optimization_barrier((swap(given), swap(to_a), across(to_b)))
+    last = lambda grad: call(last_kernel, 4, [((4, 128, 128), F32)], [((512, 384), F32)])(
+        side, grad, weight, from_a, from_b
     )[0]
-    grad_w_hidden, grad_w_rain, grad_bias = sum_everywhere(side, kept, given, swap)
+    grad_hidden, grad_w_hidden, grad_w_rain, grad_bias = sum_everywhere(
+        side, kept, got, swap, (grad0, last)
+    )
     return (
         final[None],
         grad_hidden[None],
         grad_w_hidden.reshape(hidden_weight.shape),
-        grad_w_rain.reshape(rain_weight.shape),
+        grad_w_rain,
         grad_bias.reshape(gate_bias.shape),
     )
 

time: 126 us -> 122 us (0.968)
  waiting for transfers between devices: 11.1 us -> 6.82 us
  local copies, waits for them, and re-layouts: 8.21 us -> 6.04 us
  starting transfers between devices: 16.5 us -> 18.3 us
  blocking collectives: 55.5 us -> 56.9 us
    ppermute x6, waiting for transfers between devices: 3.16 us -> 0.02 us  [on_device(): swap = lambda x: lax.ppermute(x, 'space', near)]
    ppermute x4, starting transfers between devices: 8.72 us -> 10.7 us  [on_device(): across = lambda x: lax.ppermute(x, 'space', far)]
    reshape x1 -> x0, local copies, waits for them, and re-layouts: 1.54 us -> none  [on_device(): grad_w_rain.reshape(rain_weight.shape)]
    unnamed x28 -> x24, local copies, waits for them, and re-layouts: 4.42 us -> 3.79 us
  transfers between devices with their start and end apart: 10 -> 10, of which waited for: 4 -> 3; matrix products, arithmetic and copies ran while one was open for 2% -> 2% of each run, Pallas kernels for 6% -> 6%
where the time goes in v2:
time: 122 us; the launch traced here: 121 us
  blocking collectives  56.9 us (47%)
  Pallas kernels  32.6 us (27%)
  starting transfers between devices  18.3 us (15%)
  waiting for transfers between devices  6.82 us (6%)
  local copies, waits for them, and re-layouts  6.04 us (5%)
    all_to_all x1, blocking collectives, sum_everywhere(): lax.all_to_all(parts, ('space', 'event'), 0, 0, axis_index_groups=planes)  23.2 us
    all_to_all x1, blocking collectives, sum_everywhere(): lax.all_to_all(fold(parts, 8), 'space', 0, 0, axis_index_groups=columns)  20.2 us
    all_to_all x1, blocking collectives, sum_everywhere(): lax.all_to_all(fold(parts, 16), ('space', 'event'), 0, 0, axis_index_grou...  13.4 us
    ppermute x4, starting transfers between devices, on_device(): across = lambda x: lax.ppermute(x, 'space', far)  10.7 us
    ppermute x6, starting transfers between devices, on_device(): swap = lambda x: lax.ppermute(x, 'space', near)  7.65 us
    ppermute x4, waiting for transfers between devices, on_device(): across = lambda x: lax.ppermute(x, 'space', far)  6.81 us
    pallas_call x1, Pallas kernels, on_device(): call(fourth_kernel, 14, [pile, pile, ((512, 512), BF16), row, row], [((4,...  5.91 us
    pallas_call x1, Pallas kernels, on_device(): call(third_kernel, 4, [pile, pile, ((4, 128, 128), F32)], [((512, 384), F...  4.42 us
  transfers between devices with their start and end apart: 10, of which 3 were waited for; matrix products, arithmetic and copies ran while one was open for 2% of the time, Pallas kernels for 6%

profile of v2, /device:TPU:1, one launch (start us, length us, event | category | flops | bytes accessed | tf_op | source)
XLA Modules:
  0.0 121.4 jit_solution(9115588735638958288)
XLA Ops:
  0.6 1.6 %shard_map.119 = (bf16[136,128]{1,0:T(8,128)(2,1)}, bf16[136,128]{1,0:T(8,128)(2,1)}) custom-call(s32[1]{0:T(128)} %bitcast.side_ref, bf16[4,128,128]{2,1,0:T(8,128)(2,1)} %bitcast.24, bf16[2,4,4,128]{3,2,1,0:T(4,128)(2,1)} %bitcast.27), custom_call_target="tpu_custom_call" | custom-call | tf_op jit(solution)/shard_map/pallas_call | solution.py:339
  2.2 3.2 %collective-permute-start = (bf16[136,128]{1,0:T(8,128)(2,1)}, bf16[136,128]{1,0:T(8,128)(2,1)S(1)}, u32[]{:S(2)}, u32[]{:S(2)}) collective-permute-start(bf16[136,128]{1,0:T(8,128)(2,1)} %get-tuple-element.38), channel_id=1, source_target_pairs={{0,4},{4,0},{8,12},{12,8},{16,20},{20,16},{24,28},{28,24},{32,36},... | collective-permute-start | bytes 104456 | tf_op jit(solution)/shard_map/ppermute | solution.py:329
  5.5 1.9 %collective-permute-start.1 = (bf16[136,128]{1,0:T(8,128)(2,1)}, bf16[136,128]{1,0:T(8,128)(2,1)S(1)}, u32[]{:S(2)}, u32[]{:S(2)}) collective-permute-start(bf16[136,128]{1,0:T(8,128)(2,1)} %get-tuple-element.39), channel_id=1, source_target_pairs={{4,8},{12,16},{20,24},{28,32},{36,40},{44,48},{52,56},{60,64},{68,... | collective-permute-start | bytes 104456 | tf_op jit(solution)/shard_map/ppermute | solution.py:330
  8.8 2.1 %collective-permute-done.1.from_b_ref = bf16[136,128]{1,0:T(8,128)(2,1)S(1)} collective-permute-done((bf16[136,128]{1,0:T(8,128)(2,1)}, bf16[136,128]{1,0:T(8,128)(2,1)S(1)}, u32[]{:S(2)}, u32[]{:S(2)}) %collective-permute-start.1) | collective-permute-done | bytes 34848 | tf_op jit(solution)/shard_map/ppermute | solution.py:330
  11.6 4.0 %shard_map.120 = (bf16[4,128,128]{2,1,0:T(8,128)(2,1)}, bf16[128,128]{1,0:T(8,128)(2,1)}, bf16[128,128]{1,0:T(8,128)(2,1)}, f32[512,128]{1,0:T(8,128)}, f32[512,...) custom-call(s32[1]{0:T(128)} %bitcast.side_ref, ...), custom_call_target="tpu_custom_call" | custom-call | tf_op jit(solution)/shard_map/pallas_call | solution.py:340
  15.7 2.0 %collective-permute-start.3 = (bf16[128,128]{1,0:T(8,128)(2,1)}, bf16[128,128]{1,0:T(8,128)(2,1)S(1)}, u32[]{:S(2)}, u32[]{:S(2)}) collective-permute-start(bf16[128,128]{1,0:T(8,128)(2,1)} %get-tuple-element.42), channel_id=1, source_target_pairs={{4,8},{12,16},{20,24},{28,32},{36,40},{44,48},{52,56},{60,64},{68,... | collective-permute-start | bytes 98312 | tf_op jit(solution)/shard_map/ppermute | solution.py:330
  18.6 2.6 %collective-permute-done.3.from_b_ref = bf16[128,128]{1,0:T(8,128)(2,1)S(1)} collective-permute-done((bf16[128,128]{1,0:T(8,128)(2,1)}, bf16[128,128]{1,0:T(8,128)(2,1)S(1)}, u32[]{:S(2)}, u32[]{:S(2)}) %collective-permute-start.3) | collective-permute-done | bytes 32800 | tf_op jit(solution)/shard_map/ppermute | solution.py:330
  21.8 4.3 %shard_map.121 = (bf16[4,128,128]{2,1,0:T(8,128)(2,1)}, bf16[512,512]{1,0:T(8,128)(2,1)}, f32[512,128]{1,0:T(8,128)}, f32[128,128]{1,0:T(8,128)}, f32[128,128]{1,0:T(8,128)}, /*index=5*/bf16[768,384]{1,0:T(8,128)(2,1)}) custom-call(s32[1]{0:T(128)} %bitcast.side_ref, bf16[4,128,128]{2,1,0:T(8,128)(2,1)} %get-tuple-element.40.hidden_ref, ...), custom_call_target="tpu_custom_call" | custom-call | tf_op jit(solution)/shard_map/pallas_call | solution.py:350
  26.1 2.5 %collective-permute-start.5 = (f32[128,128]{1,0:T(8,128)}, f32[128,128]{1,0:T(8,128)S(1)}, u32[]{:S(2)}, u32[]{:S(2)}) collective-permute-start(f32[128,128]{1,0:T(8,128)} %get-tuple-element.53), channel_id=1, source_target_pairs={{4,8},{12,16},{20,24},{28,32},{36,40},{44,48},{52,56},{60,64},{68,... | collective-permute-start | bytes 196616 | tf_op jit(solution)/shard_map/ppermute | solution.py:330
  28.5 4.4 %shard_map.122 = (f32[2,1216,128]{2,1,0:T(8,128)}, f32[2,1216,128]{2,1,0:T(8,128)}, f32[4,128,128]{2,1,0:T(8,128)}) custom-call(s32[1]{0:T(128)} %bitcast.side_ref, bf16[512,512]{1,0:T(8,128)(2,1)} %get-tuple-element.47.grad_ref, bf16[3,384,512]{2,1,0:T(8,128)(2,1)} %bitcast.17, bf16[768,384]{1,0:T(8,128)(2,1)} %get-tuple-element.48.wide_ref, ...), custom_call_target="tpu_custom_call" | custom-call | tf_op jit(solution)/shard_map/pallas_call | solution.py:364
  33.6 5.9 %shard_map.123 = (f32[2,1216,128]{2,1,0:T(8,128)}, f32[2,1216,128]{2,1,0:T(8,128)}, bf16[512,512]{1,0:T(8,128)(2,1)}, f32[128,128]{1,0:T(8,128)}, f32[128,128]{1,0:T(8,128)}) custom-call(s32[1]{0:T(128)} %bitcast.side_ref, f32[2,1216,128]{2,1,0:T(8,128)} %get-tuple-element.49.old_kept_ref, ...), custom_call_target="tpu_custom_call", output_to_operand_aliasing={{0}: (1, {}), {1}: (2, {})} | custom-call | tf_op jit(solution)/shard_map/pallas_call | solution.py:367
  40.0 4.3 %collective-permute-start.8 = (f32[128,128]{1,0:T(8,128)}, f32[128,128]{1,0:T(8,128)S(1)}, u32[]{:S(2)}, u32[]{:S(2)}) collective-permute-start(f32[128,128]{1,0:T(8,128)} %get-tuple-element.61), channel_id=1, source_target_pairs={{4,8},{12,16},{20,24},{28,32},{36,40},{44,48},{52,56},{60,64},{68,... | collective-permute-start | bytes 196616 | tf_op jit(solution)/shard_map/ppermute | solution.py:330
  44.3 2.1 %collective-permute-done.8.from_b_ref = f32[128,128]{1,0:T(8,128)S(1)} collective-permute-done((f32[128,128]{1,0:T(8,128)}, f32[128,128]{1,0:T(8,128)S(1)}, u32[]{:S(2)}, u32[]{:S(2)}) %collective-permute-start.8) | collective-permute-done | bytes 65568 | tf_op jit(solution)/shard_map/ppermute | solution.py:330
  46.5 1.1 copy-done.1
  47.6 2.6 %shard_map.124 = bf16[16,152,128]{2,1,0:T(8,128)(2,1)} custom-call(s32[1]{0:T(128)} %bitcast.side_ref, f32[2,1216,128]{2,1,0:T(8,128)} %get-tuple-element.58.kept_ref, f32[2,1216,128]{2,1,0:T(8,128)} %copy-done.1), custom_call_target="tpu_custom_call" | custom-call | tf_op jit(solution)/shard_map/pallas_call | solution.py:310
  50.2 23.2 %all_to_all.15.parts_ref = bf16[16,152,128]{2,1,0:T(8,128)(2,1)} all-to-all(bf16[16,152,128]{2,1,0:T(8,128)(2,1)} %shard_map.124), channel_id=1, replica_groups={{0,1,2,3,8,9,10,11,16,17,18,19,24,25,26,27},{4,5,6,7,12,13,14,15,20,21,..., dimensions={0} | all-to-all | bytes 1245184 | tf_op jit(solution)/shard_map/all_to_all | solution.py:311
  73.3 1.9 %shard_map.125 = bf16[8,152,128]{2,1,0:T(8,128)(2,1)} custom-call(s32[1]{0:T(128)} %bitcast.side_ref, bf16[16,152,128]{2,1,0:T(8,128)(2,1)} %all_to_all.15.parts_ref), custom_call_target="tpu_custom_call" | custom-call | tf_op jit(solution)/shard_map/pallas_call | solution.py:309
  75.2 20.2 %all_to_all.16.parts_ref = bf16[8,152,128]{2,1,0:T(8,128)(2,1)} all-to-all(bf16[8,152,128]{2,1,0:T(8,128)(2,1)} %shard_map.125), channel_id=1, replica_groups={{0,32,64,96,128,160,192,224},{4,36,68,100,132,164,196,228},{8,40,72,104..., dimensions={0} | all-to-all | bytes 622592 | tf_op jit(solution)/shard_map/all_to_all | solution.py:312
  95.5 1.9 %shard_map.126 = bf16[16,152,128]{2,1,0:T(8,128)(2,1)} custom-call(s32[1]{0:T(128)} %bitcast.side_ref, bf16[8,152,128]{2,1,0:T(8,128)(2,1)} %all_to_all.16.parts_ref), custom_call_target="tpu_custom_call" | custom-call | tf_op jit(solution)/shard_map/pallas_call | solution.py:309
  97.3 13.4 %all_to_all.17 = bf16[16,152,128]{2,1,0:T(8,128)(2,1)S(1)} all-to-all(bf16[16,152,128]{2,1,0:T(8,128)(2,1)} %shard_map.126), channel_id=1, replica_groups={{0,1,2,3,8,9,10,11,16,17,18,19,24,25,26,27},{4,5,6,7,12,13,14,15,20,21,..., dimensions={0} | all-to-all | bytes 1245184 | tf_op jit(solution)/shard_map/all_to_all | solution.py:313
  110.8 3.8 %collective-permute-start.9 = (bf16[2,1216,128]{2,1,0:T(8,128)(2,1)S(1)}, bf16[2,1216,128]{2,1,0:T(8,128)(2,1)S(1)}, u32[]{:S(2)}, u32[]{:S(2)}) collective-permute-start(bf16[2,1216,128]{2,1,0:T(8,128)(2,1)S(1)} %bitcast.20), channel_id=1, source_target_pairs={{0,4},{4,0},{8,12},{12,8},{16,20},{20,16},{24,28},{28,24},{32,36},... | collective-permute-start | bytes 1867784 | tf_op jit(solution)/shard_map/ppermute | solution.py:329
  114.6 3.0 %shard_map.127 = f32[4,128,128]{2,1,0:T(8,128)} custom-call(s32[1]{0:T(128)} %bitcast.side_ref, bf16[512,512]{1,0:T(8,128)(2,1)} %get-tuple-element.64.grad_ref, bf16[3,384,512]{2,1,0:T(8,128)(2,1)} %bitcast.19, f32[128,128]{1,0:T(8,128)} %copy-done.6, f32[128,128]{1,0:T(8,128)} %copy-done.7), custom_call_target="tpu_custom_call" | custom-call | tf_op jit(solution)/shard_map/pallas_call | solution.py:378
  117.6 0.8 copy-done.2
  118.4 3.0 %shard_map.128 = (f32[1152,512]{1,0:T(8,128)}, f32[9,4,512]{2,1,0:T(4,128)}, f32[1,512]{1,0:T(1,128)}) custom-call(s32[1]{0:T(128)} %bitcast.side_ref, bf16[2,1216,128]{2,1,0:T(8,128)(2,1)} %bitcast.21, bf16[2,1216,128]{2,1,0:T(8,128)(2,1)} %copy-done.2), custom_call_target="tpu_custom_call" | custom-call | tf_op jit(solution)/shard_map/pallas_call | solution.py:317
  (36 shorter events, 4.8 us)
Async XLA Ops:
  0.6 17.1 %copy-start.3 = (f32[1,2,4,128,128]{4,3,2,1,0:T(8,128)S(1)}, f32[1,2,4,128,128]{4,3,2,1,0:T(8,128)}, u32[]{:S(2)}) copy-start(f32[1,2,4,128,128]{4,3,2,1,0:T(8,128)} %param.15) | copy-start | bytes 1572868
  2.2 6.6 %collective-permute-start = (bf16[136,128]{1,0:T(8,128)(2,1)}, bf16[136,128]{1,0:T(8,128)(2,1)S(1)}, u32[]{:S(2)}, u32[]{:S(2)}) collective-permute-start(bf16[136,128]{1,0:T(8,128)(2,1)} %get-tuple-element.38), channel_id=1, source_target_pairs={{0,4},{4,0},{8,12},{12,8},{16,20},{20,16},{24,28},{28,24},{32,36},... | collective-permute-start | bytes 104456 | tf_op jit(solution)/shard_map/ppermute | solution.py:329
  5.5 5.5 %collective-permute-start.1 = (bf16[136,128]{1,0:T(8,128)(2,1)}, bf16[136,128]{1,0:T(8,128)(2,1)S(1)}, u32[]{:S(2)}, u32[]{:S(2)}) collective-permute-start(bf16[136,128]{1,0:T(8,128)(2,1)} %get-tuple-element.39), channel_id=1, source_target_pairs={{4,8},{12,16},{20,24},{28,32},{36,40},{44,48},{52,56},{60,64},{68,... | collective-permute-start | bytes 104456 | tf_op jit(solution)/shard_map/ppermute | solution.py:330
  8.8 2.1 %copy-start.8 = (bf16[136,128]{1,0:T(8,128)(2,1)}, bf16[136,128]{1,0:T(8,128)(2,1)S(1)}, u32[]{:S(2)}) copy-start(bf16[136,128]{1,0:T(8,128)(2,1)S(1)} %collective-permute-done.from_a_ref) | copy-start | bytes 104452
  10.9 0.6 copy-start.9
  15.6 3.0 %collective-permute-start.2 = (bf16[128,128]{1,0:T(8,128)(2,1)}, bf16[128,128]{1,0:T(8,128)(2,1)S(1)}, u32[]{:S(2)}, u32[]{:S(2)}) collective-permute-start(bf16[128,128]{1,0:T(8,128)(2,1)} %get-tuple-element.41), channel_id=1, source_target_pairs={{0,4},{4,0},{8,12},{12,8},{16,20},{20,16},{24,28},{28,24},{32,36},... | collective-permute-start | bytes 98312 | tf_op jit(solution)/shard_map/ppermute | solution.py:329
  15.7 5.4 %collective-permute-start.3 = (bf16[128,128]{1,0:T(8,128)(2,1)}, bf16[128,128]{1,0:T(8,128)(2,1)S(1)}, u32[]{:S(2)}, u32[]{:S(2)}) collective-permute-start(bf16[128,128]{1,0:T(8,128)(2,1)} %get-tuple-element.42), channel_id=1, source_target_pairs={{4,8},{12,16},{20,24},{28,32},{36,40},{44,48},{52,56},{60,64},{68,... | collective-permute-start | bytes 98312 | tf_op jit(solution)/shard_map/ppermute | solution.py:330
  18.6 2.6 %copy-start.10 = (bf16[128,128]{1,0:T(8,128)(2,1)}, bf16[128,128]{1,0:T(8,128)(2,1)S(1)}, u32[]{:S(2)}) copy-start(bf16[128,128]{1,0:T(8,128)(2,1)S(1)} %collective-permute-done.2.from_a_ref) | copy-start | bytes 98308
  21.1 0.6 copy-start.11
  26.0 6.9 %collective-permute-start.4 = (f32[128,128]{1,0:T(8,128)}, f32[128,128]{1,0:T(8,128)S(1)}, u32[]{:S(2)}, u32[]{:S(2)}) collective-permute-start(f32[128,128]{1,0:T(8,128)} %get-tuple-element.52), channel_id=1, source_target_pairs={{0,4},{4,0},{8,12},{12,8},{16,20},{20,16},{24,28},{28,24},{32,36},... | collective-permute-start | bytes 196616 | tf_op jit(solution)/shard_map/ppermute | solution.py:329
  26.1 6.9 %collective-permute-start.5 = (f32[128,128]{1,0:T(8,128)}, f32[128,128]{1,0:T(8,128)S(1)}, u32[]{:S(2)}, u32[]{:S(2)}) collective-permute-start(f32[128,128]{1,0:T(8,128)} %get-tuple-element.53), channel_id=1, source_target_pairs={{4,8},{12,16},{20,24},{28,32},{36,40},{44,48},{52,56},{60,64},{68,... | collective-permute-start | bytes 196616 | tf_op jit(solution)/shard_map/ppermute | solution.py:330
  33.0 0.6 copy-start.4
  33.0 0.6 copy-start.5
  39.5 7.0 %collective-permute-start.6 = (f32[2,1216,128]{2,1,0:T(8,128)}, f32[2,1216,128]{2,1,0:T(8,128)S(1)}, u32[]{:S(2)}, u32[]{:S(2)}) collective-permute-start(f32[2,1216,128]{2,1,0:T(8,128)} %get-tuple-element.59), channel_id=1, source_target_pairs={{0,4},{4,0},{8,12},{12,8},{16,20},{20,16},{24,28},{28,24},{32,36},... | collective-permute-start | bytes 3735560 | tf_op jit(solution)/shard_map/ppermute | solution.py:329
  39.5 4.8 %collective-permute-start.7 = (f32[128,128]{1,0:T(8,128)}, f32[128,128]{1,0:T(8,128)S(1)}, u32[]{:S(2)}, u32[]{:S(2)}) collective-permute-start(f32[128,128]{1,0:T(8,128)} %get-tuple-element.60), channel_id=1, source_target_pairs={{0,4},{4,0},{8,12},{12,8},{16,20},{20,16},{24,28},{28,24},{32,36},... | collective-permute-start | bytes 196616 | tf_op jit(solution)/shard_map/ppermute | solution.py:329
  40.0 6.4 %collective-permute-start.8 = (f32[128,128]{1,0:T(8,128)}, f32[128,128]{1,0:T(8,128)S(1)}, u32[]{:S(2)}, u32[]{:S(2)}) collective-permute-start(f32[128,128]{1,0:T(8,128)} %get-tuple-element.61), channel_id=1, source_target_pairs={{4,8},{12,16},{20,24},{28,32},{36,40},{44,48},{52,56},{60,64},{68,... | collective-permute-start | bytes 196616 | tf_op jit(solution)/shard_map/ppermute | solution.py:330
  44.3 66.4 %copy-start.6 = (f32[128,128]{1,0:T(8,128)}, f32[128,128]{1,0:T(8,128)S(1)}, u32[]{:S(2)}) copy-start(f32[128,128]{1,0:T(8,128)S(1)} %collective-permute-done.7.from_a_ref) | copy-start | bytes 196612
  46.5 64.3 %copy-start.7 = (f32[128,128]{1,0:T(8,128)}, f32[128,128]{1,0:T(8,128)S(1)}, u32[]{:S(2)}) copy-start(f32[128,128]{1,0:T(8,128)S(1)} %collective-permute-done.8.from_b_ref) | copy-start | bytes 196612
  46.5 1.1 copy-start.1
  110.8 6.8 %copy-start = (bf16[16,152,128]{2,1,0:T(8,128)(2,1)}, bf16[16,152,128]{2,1,0:T(8,128)(2,1)S(1)}, u32[]{:S(2)}) copy-start(bf16[16,152,128]{2,1,0:T(8,128)(2,1)S(1)} %all_to_all.17) | copy-start | bytes 1867780
  110.8 6.8 %collective-permute-start.9 = (bf16[2,1216,128]{2,1,0:T(8,128)(2,1)S(1)}, bf16[2,1216,128]{2,1,0:T(8,128)(2,1)S(1)}, u32[]{:S(2)}, u32[]{:S(2)}) collective-permute-start(bf16[2,1216,128]{2,1,0:T(8,128)(2,1)S(1)} %bitcast.20), channel_id=1, source_target_pairs={{0,4},{4,0},{8,12},{12,8},{16,20},{20,16},{24,28},{28,24},{32,36},... | collective-permute-start | bytes 1867784 | tf_op jit(solution)/shard_map/ppermute | solution.py:329
  117.6 0.8 copy-start.2

commit v3 on v2

--- a/solution.py
+++ b/solution.py
@@ -14,7 +14,8 @@
 TN = (((0,), (0,)), ((), ()))
 SMEM = pl.BlockSpec(memory_space=pltpu.SMEM)
 VMEM = pl.BlockSpec(memory_space=pltpu.VMEM)
-LINES = 1216
+LINES = 1200
+PIECE = 24
 
 
 def dot(a, b, dims):
@@ -210,10 +211,10 @@
                 out_ref[part, spot, :] = piece
         total = dot(taps_ref[...], grad, NN)
         for part in range(2):
-            piece = total[:, part * 128 : part * 128 + 128]
+            piece = total[0 : LINES - 1152, part * 128 : part * 128 + 128]
             if old_ref is not None:
-                piece = piece + old_ref[part, 1152:1216, :]
-            out_ref[part, 1152:1216, :] = piece
+                piece = piece + old_ref[part, 1152:LINES, :]
+            out_ref[part, 1152:LINES, :] = piece
 
 
 def third_kernel(
@@ -266,12 +267,15 @@
 
 
 def pair_kernel(side_ref, kept_ref, got_ref, out_ref):
+    live = LINES // PIECE
     for part in range(2):
-        for piece in range(8):
-            spot = slice(piece * 152, piece * 152 + 152)
-            out_ref[part * 8 + piece] = (kept_ref[part, spot, :] + got_ref[part, spot, :]).astype(
-                BF16
-            )
+        for piece in range(live):
+            spot = slice(piece * PIECE, piece * PIECE + PIECE)
+            out_ref[part * live + piece] = (
+                kept_ref[part, spot, :] + got_ref[part, spot, :]
+            ).astype(BF16)
+    for piece in range(2 * live, out_ref.shape[0]):
+        out_ref[piece] = jnp.zeros((PIECE, 128), BF16)
 
 
 def fold_kernel(side_ref, parts_ref, out_ref):
@@ -287,31 +291,28 @@
     for half, source_ref in ((side_ref[0], mine_ref), (1 - side_ref[0], other_ref)):
         for part in range(2):
             lanes = pl.ds(pl.multiple_of(half * 256 + part * 128, 128), 128)
-            hidden_ref[:, lanes] = source_ref[part, 0:1152, :].astype(F32)
-            tail = source_ref[part, 1152:1216, :].astype(F32)
+            first = part * LINES
+            hidden_ref[:, lanes] = source_ref[first : first + 1152, :].astype(F32)
+            tail = source_ref[first + 1152 : first + LINES, :].astype(F32)
             for tap in range(9):
                 rain_ref[tap, :, lanes] = tail[tap * 4 : tap * 4 + 4]
             bias_ref[:, lanes] = tail[36:37]
 
 
-def device_groups(deep, wide, across):
-    planes = [
-        [((z * wide + y) * 2 + core) * across + x for y in range(wide) for x in range(across)]
-        for z in range(deep)
+def device_groups(chips, across):
+    return [
+        [(chip * 2 + core) * across + x for chip in range(chips) for x in range(across)]
         for core in range(2)
     ]
-    columns = [[z * wide * 2 + low for z in range(deep)] for low in range(wide * 2)]
-    return (planes, columns)
 
 
 def sum_everywhere(side, kept, got, swap, beside):
-    planes, columns = device_groups(8, 4, 4)
-    fold = lambda parts, copies: call(fold_kernel, 1, [((copies, 152, 128), BF16)])(side, parts)[0]
-    parts = call(pair_kernel, 2, [((16, 152, 128), BF16)])(side, kept, got)[0]
-    parts = lax.all_to_all(parts, ("space", "event"), 0, 0, axis_index_groups=planes)
-    parts = lax.all_to_all(fold(parts, 8), "space", 0, 0, axis_index_groups=columns)
-    parts = lax.all_to_all(fold(parts, 16), ("space", "event"), 0, 0, axis_index_groups=planes)
-    mine = parts.reshape(2, LINES, 128)
+    groups = device_groups(32, 4)
+    pieces = [((128, PIECE, 128), BF16)]
+    spread = lambda x: lax.all_to_all(x, ("space", "event"), 0, 0, axis_index_groups=groups)
+    parts = spread(call(pair_kernel, 2, pieces)(side, kept, got)[0])
+    parts = spread(call(fold_kernel, 1, pieces)(side, parts)[0])
+    mine = parts.reshape(128 * PIECE, 128)
     mine, held = lax.optimization_barrier((mine, beside[0]))
     other, hidden = swap(mine), beside[1](held)
     return hidden, *call(

time: 122 us -> 141 us (1.16)
  blocking collectives: 56.9 us -> 75.9 us
    all_to_all x3 -> x2, blocking collectives: 56.9 us -> 75.9 us  [sum_everywhere(): lax.all_to_all(x, ('space', 'event'), 0, 0, axis_index_groups=groups)]
    pallas_call x3 -> x2, Pallas kernels: 6.35 us -> 4.88 us  [the longest x1 2.67 us: sum_everywhere(): parts = spread(call(pair_kernel, 2, pieces)(side, kept, got)[0])]
  transfers between devices with their start and end apart: 10 -> 10, of which waited for: 3 -> 3; matrix products, arithmetic and copies ran while one was open for 2% -> 2% of each run, Pallas kernels for 6% -> 5%
where the time goes in v3:
time: 141 us; the launch traced here: 140 us
  blocking collectives  75.9 us (54%)
  Pallas kernels  31.2 us (22%)
  starting transfers between devices  19.6 us (14%)
  waiting for transfers between devices  6.82 us (5%)
  local copies, waits for them, and re-layouts  6.09 us (4%)
    all_to_all x2, blocking collectives, sum_everywhere(): lax.all_to_all(x, ('space', 'event'), 0, 0, axis_index_groups=groups)  75.9 us
    ppermute x4, starting transfers between devices, on_device(): across = lambda x: lax.ppermute(x, 'space', far)  10.7 us
    ppermute x6, starting transfers between devices, on_device(): swap = lambda x: lax.ppermute(x, 'space', near)  8.92 us
    ppermute x4, waiting for transfers between devices, on_device(): across = lambda x: lax.ppermute(x, 'space', far)  6.81 us
    pallas_call x1, Pallas kernels, on_device(): call(fourth_kernel, 14, [pile, pile, ((512, 512), BF16), row, row], [((4,...  5.9 us
    pallas_call x1, Pallas kernels, on_device(): call(third_kernel, 4, [pile, pile, ((4, 128, 128), F32)], [((512, 384), F...  4.4 us
    pallas_call x1, Pallas kernels, on_device(): call(second_kernel, 10, [((4, 128, 128), BF16), ((512, 512), BF16), ((512...  4.29 us
    pallas_call x1, Pallas kernels, on_device(): call(first_kernel, 9, [((4, 128, 128), BF16), ((128, 128), BF16), ((128,...  4.03 us
  transfers between devices with their start and end apart: 10, of which 3 were waited for; matrix products, arithmetic and copies ran while one was open for 2% of the time, Pallas kernels for 5%

profile of v3, /device:TPU:1, one launch (start us, length us, event | category | flops | bytes accessed | tf_op | source)
XLA Modules:
  0.0 140.3 jit_solution(7907751707398333360)
XLA Ops:
  0.6 1.6 %shard_map.119 = (bf16[136,128]{1,0:T(8,128)(2,1)}, bf16[136,128]{1,0:T(8,128)(2,1)}) custom-call(s32[1]{0:T(128)} %bitcast.side_ref, bf16[4,128,128]{2,1,0:T(8,128)(2,1)} %bitcast.24, bf16[2,4,4,128]{3,2,1,0:T(4,128)(2,1)} %bitcast.27), custom_call_target="tpu_custom_call" | custom-call | tf_op jit(solution)/shard_map/pallas_call | solution.py:340
  2.2 3.2 %collective-permute-start = (bf16[136,128]{1,0:T(8,128)(2,1)}, bf16[136,128]{1,0:T(8,128)(2,1)S(1)}, u32[]{:S(2)}, u32[]{:S(2)}) collective-permute-start(bf16[136,128]{1,0:T(8,128)(2,1)} %get-tuple-element.38), channel_id=1, source_target_pairs={{0,4},{4,0},{8,12},{12,8},{16,20},{20,16},{24,28},{28,24},{32,36},... | collective-permute-start | bytes 104456 | tf_op jit(solution)/shard_map/ppermute | solution.py:330
  5.5 1.9 %collective-permute-start.1 = (bf16[136,128]{1,0:T(8,128)(2,1)}, bf16[136,128]{1,0:T(8,128)(2,1)S(1)}, u32[]{:S(2)}, u32[]{:S(2)}) collective-permute-start(bf16[136,128]{1,0:T(8,128)(2,1)} %get-tuple-element.39), channel_id=1, source_target_pairs={{4,8},{12,16},{20,24},{28,32},{36,40},{44,48},{52,56},{60,64},{68,... | collective-permute-start | bytes 104456 | tf_op jit(solution)/shard_map/ppermute | solution.py:331
  7.4 0.8 reshape.32
  8.8 2.1 %collective-permute-done.1.from_b_ref = bf16[136,128]{1,0:T(8,128)(2,1)S(1)} collective-permute-done((bf16[136,128]{1,0:T(8,128)(2,1)}, bf16[136,128]{1,0:T(8,128)(2,1)S(1)}, u32[]{:S(2)}, u32[]{:S(2)}) %collective-permute-start.1) | collective-permute-done | bytes 34848 | tf_op jit(solution)/shard_map/ppermute | solution.py:331
  11.6 4.0 %shard_map.120 = (bf16[4,128,128]{2,1,0:T(8,128)(2,1)}, bf16[128,128]{1,0:T(8,128)(2,1)}, bf16[128,128]{1,0:T(8,128)(2,1)}, f32[512,128]{1,0:T(8,128)}, f32[512,...) custom-call(s32[1]{0:T(128)} %bitcast.side_ref, ...), custom_call_target="tpu_custom_call" | custom-call | tf_op jit(solution)/shard_map/pallas_call | solution.py:341
  15.7 2.0 %collective-permute-start.3 = (bf16[128,128]{1,0:T(8,128)(2,1)}, bf16[128,128]{1,0:T(8,128)(2,1)S(1)}, u32[]{:S(2)}, u32[]{:S(2)}) collective-permute-start(bf16[128,128]{1,0:T(8,128)(2,1)} %get-tuple-element.42), channel_id=1, source_target_pairs={{4,8},{12,16},{20,24},{28,32},{36,40},{44,48},{52,56},{60,64},{68,... | collective-permute-start | bytes 98312 | tf_op jit(solution)/shard_map/ppermute | solution.py:331
  17.7 0.8 slice_bitcast_fusion
  18.6 2.6 %collective-permute-done.3.from_b_ref = bf16[128,128]{1,0:T(8,128)(2,1)S(1)} collective-permute-done((bf16[128,128]{1,0:T(8,128)(2,1)}, bf16[128,128]{1,0:T(8,128)(2,1)S(1)}, u32[]{:S(2)}, u32[]{:S(2)}) %collective-permute-start.3) | collective-permute-done | bytes 32800 | tf_op jit(solution)/shard_map/ppermute | solution.py:331
  21.7 4.3 %shard_map.121 = (bf16[4,128,128]{2,1,0:T(8,128)(2,1)}, bf16[512,512]{1,0:T(8,128)(2,1)}, f32[512,128]{1,0:T(8,128)}, f32[128,128]{1,0:T(8,128)}, f32[128,128]{1,0:T(8,128)}, /*index=5*/bf16[768,384]{1,0:T(8,128)(2,1)}) custom-call(s32[1]{0:T(128)} %bitcast.side_ref, bf16[4,128,128]{2,1,0:T(8,128)(2,1)} %get-tuple-element.40.hidden_ref, ...), custom_call_target="tpu_custom_call" | custom-call | tf_op jit(solution)/shard_map/pallas_call | solution.py:351
  26.0 2.5 %collective-permute-start.5 = (f32[128,128]{1,0:T(8,128)}, f32[128,128]{1,0:T(8,128)S(1)}, u32[]{:S(2)}, u32[]{:S(2)}) collective-permute-start(f32[128,128]{1,0:T(8,128)} %get-tuple-element.53), channel_id=1, source_target_pairs={{4,8},{12,16},{20,24},{28,32},{36,40},{44,48},{52,56},{60,64},{68,... | collective-permute-start | bytes 196616 | tf_op jit(solution)/shard_map/ppermute | solution.py:331
  28.5 4.4 %shard_map.122 = (f32[2,1200,128]{2,1,0:T(8,128)}, f32[2,1200,128]{2,1,0:T(8,128)}, f32[4,128,128]{2,1,0:T(8,128)}) custom-call(s32[1]{0:T(128)} %bitcast.side_ref, bf16[512,512]{1,0:T(8,128)(2,1)} %get-tuple-element.47.grad_ref, bf16[3,384,512]{2,1,0:T(8,128)(2,1)} %bitcast.17, bf16[768,384]{1,0:T(8,128)(2,1)} %get-tuple-element.48.wide_ref, ...), custom_call_target="tpu_custom_call" | custom-call | tf_op jit(solution)/shard_map/pallas_call | solution.py:365
  33.6 5.9 %shard_map.123 = (f32[2,1200,128]{2,1,0:T(8,128)}, f32[2,1200,128]{2,1,0:T(8,128)}, bf16[512,512]{1,0:T(8,128)(2,1)}, f32[128,128]{1,0:T(8,128)}, f32[128,128]{1,0:T(8,128)}) custom-call(s32[1]{0:T(128)} %bitcast.side_ref, f32[2,1200,128]{2,1,0:T(8,128)} %get-tuple-element.49.old_kept_ref, ...), custom_call_target="tpu_custom_call", output_to_operand_aliasing={{0}: (1, {}), {1}: (2, {})} | custom-call | tf_op jit(solution)/shard_map/pallas_call | solution.py:368
  40.0 4.3 %collective-permute-start.8 = (f32[128,128]{1,0:T(8,128)}, f32[128,128]{1,0:T(8,128)S(1)}, u32[]{:S(2)}, u32[]{:S(2)}) collective-permute-start(f32[128,128]{1,0:T(8,128)} %get-tuple-element.61), channel_id=1, source_target_pairs={{4,8},{12,16},{20,24},{28,32},{36,40},{44,48},{52,56},{60,64},{68,... | collective-permute-start | bytes 196616 | tf_op jit(solution)/shard_map/ppermute | solution.py:331
  44.3 2.1 %collective-permute-done.8.from_b_ref = f32[128,128]{1,0:T(8,128)S(1)} collective-permute-done((f32[128,128]{1,0:T(8,128)}, f32[128,128]{1,0:T(8,128)S(1)}, u32[]{:S(2)}, u32[]{:S(2)}) %collective-permute-start.8) | collective-permute-done | bytes 65568 | tf_op jit(solution)/shard_map/ppermute | solution.py:331
  46.4 1.1 copy-done.1
  47.5 2.7 %shard_map.124 = bf16[128,24,128]{2,1,0:T(8,128)(2,1)} custom-call(s32[1]{0:T(128)} %bitcast.side_ref, f32[2,1200,128]{2,1,0:T(8,128)} %get-tuple-element.58.kept_ref, f32[2,1200,128]{2,1,0:T(8,128)} %copy-done.1), custom_call_target="tpu_custom_call" | custom-call | tf_op jit(solution)/shard_map/pallas_call | solution.py:313
  50.2 46.9 %all_to_all.10.parts_ref = bf16[128,24,128]{2,1,0:T(8,128)(2,1)} all-to-all(bf16[128,24,128]{2,1,0:T(8,128)(2,1)} %shard_map.124), channel_id=1, replica_groups={{0,1,2,3,8,9,10,11,16,17,18,19,24,25,26,27,32,33,34,35,40,41,42,43,48,4..., dimensions={0} | all-to-all | bytes 1572864 | tf_op jit(solution)/shard_map/all_to_all | solution.py:312
  97.1 2.2 %shard_map.125 = bf16[128,24,128]{2,1,0:T(8,128)(2,1)} custom-call(s32[1]{0:T(128)} %bitcast.side_ref, bf16[128,24,128]{2,1,0:T(8,128)(2,1)} %all_to_all.10.parts_ref), custom_call_target="tpu_custom_call" | custom-call | tf_op jit(solution)/shard_map/pallas_call | solution.py:314
  99.3 28.9 %all_to_all.11 = bf16[128,24,128]{2,1,0:T(8,128)(2,1)S(1)} all-to-all(bf16[128,24,128]{2,1,0:T(8,128)(2,1)} %shard_map.125), channel_id=1, replica_groups={{0,1,2,3,8,9,10,11,16,17,18,19,24,25,26,27,32,33,34,35,40,41,42,43,48,4..., dimensions={0} | all-to-all | bytes 1572864 | tf_op jit(solution)/shard_map/all_to_all | solution.py:312
  128.2 5.1 %collective-permute-start.9 = (bf16[3072,128]{1,0:T(8,128)(2,1)S(1)}, bf16[3072,128]{1,0:T(8,128)(2,1)S(1)}, u32[]{:S(2)}, u32[]{:S(2)}) collective-permute-start(bf16[3072,128]{1,0:T(8,128)(2,1)S(1)} %bitcast.20), channel_id=1, source_target_pairs={{0,4},{4,0},{8,12},{12,8},{16,20},{20,16},{24,28},{28,24},{32,36},... | collective-permute-start | bytes 2359304 | tf_op jit(solution)/shard_map/ppermute | solution.py:330
  133.3 3.0 %shard_map.126 = f32[4,128,128]{2,1,0:T(8,128)} custom-call(s32[1]{0:T(128)} %bitcast.side_ref, bf16[512,512]{1,0:T(8,128)(2,1)} %get-tuple-element.64.grad_ref, bf16[3,384,512]{2,1,0:T(8,128)(2,1)} %bitcast.19, f32[128,128]{1,0:T(8,128)} %copy-done.6, f32[128,128]{1,0:T(8,128)} %copy-done.7), custom_call_target="tpu_custom_call" | custom-call | tf_op jit(solution)/shard_map/pallas_call | solution.py:379
  136.3 0.9 copy-done.2
  137.2 3.1 %shard_map.127 = (f32[1152,512]{1,0:T(8,128)}, f32[9,4,512]{2,1,0:T(4,128)}, f32[1,512]{1,0:T(1,128)}) custom-call(s32[1]{0:T(128)} %bitcast.side_ref, bf16[3072,128]{1,0:T(8,128)(2,1)} %bitcast.21, bf16[3072,128]{1,0:T(8,128)(2,1)} %copy-done.2), custom_call_target="tpu_custom_call" | custom-call | tf_op jit(solution)/shard_map/pallas_call | solution.py:318
  (34 shorter events, 3.1 us)
Async XLA Ops:
  0.6 17.1 %copy-start.3 = (f32[1,2,4,128,128]{4,3,2,1,0:T(8,128)S(1)}, f32[1,2,4,128,128]{4,3,2,1,0:T(8,128)}, u32[]{:S(2)}) copy-start(f32[1,2,4,128,128]{4,3,2,1,0:T(8,128)} %param.15) | copy-start | bytes 1572868
  2.2 6.6 %collective-permute-start = (bf16[136,128]{1,0:T(8,128)(2,1)}, bf16[136,128]{1,0:T(8,128)(2,1)S(1)}, u32[]{:S(2)}, u32[]{:S(2)}) collective-permute-start(bf16[136,128]{1,0:T(8,128)(2,1)} %get-tuple-element.38), channel_id=1, source_target_pairs={{0,4},{4,0},{8,12},{12,8},{16,20},{20,16},{24,28},{28,24},{32,36},... | collective-permute-start | bytes 104456 | tf_op jit(solution)/shard_map/ppermute | solution.py:330
  5.5 5.5 %collective-permute-start.1 = (bf16[136,128]{1,0:T(8,128)(2,1)}, bf16[136,128]{1,0:T(8,128)(2,1)S(1)}, u32[]{:S(2)}, u32[]{:S(2)}) collective-permute-start(bf16[136,128]{1,0:T(8,128)(2,1)} %get-tuple-element.39), channel_id=1, source_target_pairs={{4,8},{12,16},{20,24},{28,32},{36,40},{44,48},{52,56},{60,64},{68,... | collective-permute-start | bytes 104456 | tf_op jit(solution)/shard_map/ppermute | solution.py:331
  8.8 2.1 %copy-start.8 = (bf16[136,128]{1,0:T(8,128)(2,1)}, bf16[136,128]{1,0:T(8,128)(2,1)S(1)}, u32[]{:S(2)}) copy-start(bf16[136,128]{1,0:T(8,128)(2,1)S(1)} %collective-permute-done.from_a_ref) | copy-start | bytes 104452
  10.9 0.6 copy-start.9
  15.6 3.0 %collective-permute-start.2 = (bf16[128,128]{1,0:T(8,128)(2,1)}, bf16[128,128]{1,0:T(8,128)(2,1)S(1)}, u32[]{:S(2)}, u32[]{:S(2)}) collective-permute-start(bf16[128,128]{1,0:T(8,128)(2,1)} %get-tuple-element.41), channel_id=1, source_target_pairs={{0,4},{4,0},{8,12},{12,8},{16,20},{20,16},{24,28},{28,24},{32,36},... | collective-permute-start | bytes 98312 | tf_op jit(solution)/shard_map/ppermute | solution.py:330
  15.7 5.4 %collective-permute-start.3 = (bf16[128,128]{1,0:T(8,128)(2,1)}, bf16[128,128]{1,0:T(8,128)(2,1)S(1)}, u32[]{:S(2)}, u32[]{:S(2)}) collective-permute-start(bf16[128,128]{1,0:T(8,128)(2,1)} %get-tuple-element.42), channel_id=1, source_target_pairs={{4,8},{12,16},{20,24},{28,32},{36,40},{44,48},{52,56},{60,64},{68,... | collective-permute-start | bytes 98312 | tf_op jit(solution)/shard_map/ppermute | solution.py:331
  18.6 2.6 %copy-start.10 = (bf16[128,128]{1,0:T(8,128)(2,1)}, bf16[128,128]{1,0:T(8,128)(2,1)S(1)}, u32[]{:S(2)}) copy-start(bf16[128,128]{1,0:T(8,128)(2,1)S(1)} %collective-permute-done.2.from_a_ref) | copy-start | bytes 98308
  21.1 0.6 copy-start.11
  26.0 6.9 %collective-permute-start.4 = (f32[128,128]{1,0:T(8,128)}, f32[128,128]{1,0:T(8,128)S(1)}, u32[]{:S(2)}, u32[]{:S(2)}) collective-permute-start(f32[128,128]{1,0:T(8,128)} %get-tuple-element.52), channel_id=1, source_target_pairs={{0,4},{4,0},{8,12},{12,8},{16,20},{20,16},{24,28},{28,24},{32,36},... | collective-permute-start | bytes 196616 | tf_op jit(solution)/shard_map/ppermute | solution.py:330
  26.0 6.9 %collective-permute-start.5 = (f32[128,128]{1,0:T(8,128)}, f32[128,128]{1,0:T(8,128)S(1)}, u32[]{:S(2)}, u32[]{:S(2)}) collective-permute-start(f32[128,128]{1,0:T(8,128)} %get-tuple-element.53), channel_id=1, source_target_pairs={{4,8},{12,16},{20,24},{28,32},{36,40},{44,48},{52,56},{60,64},{68,... | collective-permute-start | bytes 196616 | tf_op jit(solution)/shard_map/ppermute | solution.py:331
  32.9 0.6 copy-start.4
  32.9 0.6 copy-start.5
  39.5 7.0 %collective-permute-start.6 = (f32[2,1200,128]{2,1,0:T(8,128)}, f32[2,1200,128]{2,1,0:T(8,128)S(1)}, u32[]{:S(2)}, u32[]{:S(2)}) collective-permute-start(f32[2,1200,128]{2,1,0:T(8,128)} %get-tuple-element.59), channel_id=1, source_target_pairs={{0,4},{4,0},{8,12},{12,8},{16,20},{20,16},{24,28},{28,24},{32,36},... | collective-permute-start | bytes 3686408 | tf_op jit(solution)/shard_map/ppermute | solution.py:330
  39.5 4.8 %collective-permute-start.7 = (f32[128,128]{1,0:T(8,128)}, f32[128,128]{1,0:T(8,128)S(1)}, u32[]{:S(2)}, u32[]{:S(2)}) collective-permute-start(f32[128,128]{1,0:T(8,128)} %get-tuple-element.60), channel_id=1, source_target_pairs={{0,4},{4,0},{8,12},{12,8},{16,20},{20,16},{24,28},{28,24},{32,36},... | collective-permute-start | bytes 196616 | tf_op jit(solution)/shard_map/ppermute | solution.py:330
  40.0 6.4 %collective-permute-start.8 = (f32[128,128]{1,0:T(8,128)}, f32[128,128]{1,0:T(8,128)S(1)}, u32[]{:S(2)}, u32[]{:S(2)}) collective-permute-start(f32[128,128]{1,0:T(8,128)} %get-tuple-element.61), channel_id=1, source_target_pairs={{4,8},{12,16},{20,24},{28,32},{36,40},{44,48},{52,56},{60,64},{68,... | collective-permute-start | bytes 196616 | tf_op jit(solution)/shard_map/ppermute | solution.py:331
  44.3 83.9 %copy-start.6 = (f32[128,128]{1,0:T(8,128)}, f32[128,128]{1,0:T(8,128)S(1)}, u32[]{:S(2)}) copy-start(f32[128,128]{1,0:T(8,128)S(1)} %collective-permute-done.7.from_a_ref) | copy-start | bytes 196612
  46.4 81.8 %copy-start.7 = (f32[128,128]{1,0:T(8,128)}, f32[128,128]{1,0:T(8,128)S(1)}, u32[]{:S(2)}) copy-start(f32[128,128]{1,0:T(8,128)S(1)} %collective-permute-done.8.from_b_ref) | copy-start | bytes 196612
  46.4 1.1 copy-start.1
  128.2 8.1 %copy-start = (bf16[128,24,128]{2,1,0:T(8,128)(2,1)}, bf16[128,24,128]{2,1,0:T(8,128)(2,1)S(1)}, u32[]{:S(2)}) copy-start(bf16[128,24,128]{2,1,0:T(8,128)(2,1)S(1)} %all_to_all.11) | copy-start | bytes 2359300
  128.2 8.1 %collective-permute-start.9 = (bf16[3072,128]{1,0:T(8,128)(2,1)S(1)}, bf16[3072,128]{1,0:T(8,128)(2,1)S(1)}, u32[]{:S(2)}, u32[]{:S(2)}) collective-permute-start(bf16[3072,128]{1,0:T(8,128)(2,1)S(1)} %bitcast.20), channel_id=1, source_target_pairs={{0,4},{4,0},{8,12},{12,8},{16,20},{20,16},{24,28},{28,24},{32,36},... | collective-permute-start | bytes 2359304 | tf_op jit(solution)/shard_map/ppermute | solution.py:330
  136.3 0.9 copy-start.2
